TPU v7x, 128 devices: a whole 4x4x4 slice. The times are simulated.
128 devices in a mesh: grp: 2 (over y_hi), row: 8 (over z, y_lo), col: 8 (over x, core).
Axes of the slice: x: 4, y: 4 (y_hi: 2, y_lo: 2; y = y_hi * 2 + y_lo), z: 4, core: 2. Of those that a mesh axis runs over, the one named last changes fastest.
Arguments:
- queries: bfloat16 [8192, 2048], P(('row', 'col'), 'grp'), parts along dimension 1, may hold values from -102 to 102
- keys: bfloat16 [8192, 256], P(('col', 'row'), 'grp'), parts along dimension 1, may hold values from -5 to 5
- values: bfloat16 [8192, 256], P(('col', 'row'), 'grp'), parts along dimension 1, may hold values from -6 to 6
- span_order: int32 [64], replicated, may hold values from 0 to 63, each once
Outputs:
- attended: float32 [8192, 2048], P(('row', 'col'), 'grp'), parts along dimension 1
There are 2 independent parts, one for each index of `grp`. A program takes and returns all parts, laid end to end along the dimension named above; an argument that names none is the same for every part. Nothing has to cross between parts.
All inputs are finite; a program needn't handle non-finite values.
Results may differ from a plain program's by a relative error of at most 0.0022.
Values may be sent and summed in bfloat16 or wider, within the bound.
No kernel may reach another device: no remote copies, remote signals or barrier semaphores. Data moves between devices by JAX's collectives and lax.ppermute only.
A program may use at most 64 MiB of HBM per device.

v0:
```python
import functools
import math

import jax
import jax.numpy as jnp
from jax import lax
from jax.experimental import pallas as pl
from jax.experimental.pallas import tpu as pltpu
from jax.sharding import PartitionSpec as P

HEADS = 8
HD = 128
SPAN = 128
ROWS = HEADS * SPAN
GROUP = 4
BLOCK = GROUP * SPAN
NEVER = -1e30
FLOOR = -1e29
FRESH = ()
SCALE = math.log2(math.e) / math.sqrt(HD)
VMEM = pltpu.VMEM
AXES = ("row", "col")


def place(z, y, x, core):
    return (z % 4 * 2 + y % 2) * 8 + x % 4 * 2 + core


def coords(index):
    row, col = divmod(index, 8)
    return row // 2, row % 2, col // 2, col % 2


def moved(to):
    return [(i, place(*to(*coords(i)))) for i in range(64)]


def along_a(step):
    return moved(lambda z, y, x, c: (z + step, y, x, c) if c == 0 else (z, y, x + step, c))


def along_b(step):
    return moved(lambda z, y, x, c: (z, y, x + step, c) if c == 0 else (z + step, y, x, c))


ACROSS_Y = moved(lambda z, y, x, c: (z, 1 - y, x, c))
ACROSS_CORE = moved(lambda z, y, x, c: (z, y, x, 1 - c))


def send(x, perm):
    return lax.ppermute(x, AXES, perm)


def whole(space=VMEM):
    return pl.BlockSpec(memory_space=space)


def limit(mib):
    return pltpu.CompilerParams(vmem_limit_bytes=mib << 20)


def cost(flops, moved_bytes, exps=0):
    return pl.CostEstimate(flops=flops, bytes_accessed=moved_bytes, transcendentals=exps)


NEAR_A = (0, -1, 1, 2)
FAR_B = (-1, 1, 2)


def ring(core, b):
    return tuple((core, a, b) for a in NEAR_A)


OWN, BESIDE = range(2)
LISTS = (
    (BESIDE, ring(0, 0) + ring(1, 0)),
    (BESIDE, ring(0, 2)),
    (BESIDE, ring(1, 2) + ring(0, -1) + ring(0, 1)),
    (BESIDE, ring(1, -1) + ring(1, 1)),
    (OWN, ring(0, 0) + ring(1, 0) + ring(0, 2) + ring(1, 2) + ring(0, -1) + ring(0, 1) + ring(1, -1) + ring(1, 1)),
)
KINDS = 48
STEPS = 127
TABLE = 8


def lists_kernel(order_ref, table_ref):
    row, col = lax.axis_index("row"), lax.axis_index("col")
    z, y, x, core = row >> 1, row & 1, col >> 1, col & 1
    orders = {}
    for other in range(2):
        there = 1 - core if other else core
        first = there == 0
        at_a, at_b = jnp.where(first, z, x), jnp.where(first, x, z)
        wide_a, wide_b = jnp.where(first, 2, 16), jnp.where(first, 16, 2)
        part_a = {a: ((at_a + a) & 3) * wide_a + there * 8 + y for a in NEAR_A}
        part_b = {b: ((at_b + b) & 3) * wide_b for b in (0, *FAR_B)}
        for b in (0, *FAR_B):
            for a in NEAR_A:
                orders[other, a, b] = order_ref[part_a[a] + part_b[b]]
    for u, (which, slots) in enumerate(LISTS):
        to_y = y if which == OWN else 1 - y
        mine = order_ref[(z * 2 + to_y) * 8 + x * 2 + core]
        used = jnp.int32(0)
        for slot, at in enumerate(slots):
            table_ref[u, used] = slot
            table_ref[u, KINDS + used] = jnp.where(orders[at] == mine, 0, -SPAN)
            used = used + (orders[at] <= mine).astype(jnp.int32)
        for extra in range(GROUP):
            table_ref[u, used + extra] = 0
            table_ref[u, KINDS + used + extra] = SPAN
        table_ref[u, STEPS] = (used + 1) >> 1


def lists(span_order):
    return pl.pallas_call(
        lists_kernel,
        out_shape=jax.ShapeDtypeStruct((TABLE, STEPS + 1), jnp.int32),
        in_specs=[whole(pltpu.SMEM)],
        out_specs=whole(pltpu.SMEM),
        compiler_params=limit(1),
        name="lists",
        cost_estimate=cost(1024, 1024),
    )(span_order)


def split_queries(queries_ref, q_ref):
    for head in range(HEADS):
        q = queries_ref[:, head * HD : (head + 1) * HD].astype(jnp.float32) * SCALE
        high = q.astype(jnp.bfloat16)
        rows = slice(head * SPAN, (head + 1) * SPAN)
        q_ref[rows, :HD] = high
        q_ref[rows, HD:] = (q - high.astype(jnp.float32)).astype(jnp.bfloat16)


def above_diagonal():
    return lax.broadcasted_iota(jnp.int32, (SPAN, SPAN), 0) - lax.broadcasted_iota(jnp.int32, (SPAN, SPAN), 1)


def keys_of(table_ref, u, kv_ref, step, columns, size):
    spans = [table_ref[u, step * GROUP + g] for g in range(size)]
    parts = [kv_ref[pl.ds(pl.multiple_of(s * SPAN, SPAN), SPAN), columns] for s in spans]
    return jnp.concatenate(parts, axis=0)


def score_step(table_ref, u, kv_ref, q_ref, step, above, s_ref, top_ref, size=GROUP):
    k = keys_of(table_ref, u, kv_ref, step, slice(0, HD), size)
    s = lax.dot_general(
        q_ref[...], jnp.concatenate([k, k], axis=1), (((1,), (1,)), ((), ())), preferred_element_type=jnp.float32
    )
    tiles = []
    for g in range(size):
        allowed = above >= table_ref[u, KINDS + step * GROUP + g]
        tile = s[:, g * SPAN : (g + 1) * SPAN].reshape(HEADS, SPAN, SPAN)
        tiles.append(jnp.where(allowed[None], tile, NEVER).reshape(ROWS, SPAN))
    s_ref[:, : size * SPAN] = jnp.concatenate(tiles, axis=1)
    top_ref[...] = functools.reduce(jnp.maximum, tiles)


def absorb_step(table_ref, u, kv_ref, step, s_ref, top_ref, m_ref, acc_ref, size=GROUP, held=None):
    top = jnp.max(top_ref[...], axis=1, keepdims=True)
    if held is FRESH:
        new = jnp.broadcast_to(jnp.maximum(top, FLOOR), (ROWS, HD))
    else:
        m_old, acc_old = held or (m_ref, acc_ref)
        old = m_old[...]
        new = jnp.maximum(old, top)
        fade = jnp.exp2(old - new)
    m_ref[...] = new
    scores = s_ref[:, : size * SPAN]
    weights = jnp.exp2(scores - jnp.concatenate([new] * size, axis=1)).astype(jnp.bfloat16)
    v = keys_of(table_ref, u, kv_ref, step, slice(HD, 2 * HD), size)
    v = jnp.concatenate([v, jnp.ones((size * SPAN, HD), jnp.bfloat16)], axis=1)
    more = jnp.dot(weights, v, preferred_element_type=jnp.float32)
    if held is FRESH:
        acc_ref[...] = more
    else:
        acc_ref[...] = acc_old[...] * jnp.concatenate([fade, fade], axis=1) + more


def steps_of(halves, most, table_ref, u, kv_ref, q_ref, state, held, s_ref, top_ref):
    m_ref, acc_ref = state
    above = above_diagonal()

    def score(step, half, size=GROUP):
        score_step(table_ref, u, kv_ref, q_ref, step, above, s_ref.at[half], top_ref.at[half], size)

    def absorb(step, half, size=GROUP, held=None):
        absorb_step(table_ref, u, kv_ref, step, s_ref.at[half], top_ref.at[half], m_ref, acc_ref, size, held)

    def keep():
        if held is FRESH:
            m_ref[...] = jnp.full((ROWS, HD), FLOOR, jnp.float32)
            acc_ref[...] = jnp.zeros((ROWS, 2 * HD), jnp.float32)
        else:
            m_ref[...] = held[0][...]
            acc_ref[...] = held[1][...]

    @pl.when(halves == 1)
    def _():
        score(0, 0, 2)
        absorb(0, 0, 2, held)

    if most <= 4:
        pl.when(halves == 0)(keep)

        @pl.when(halves == 2)
        def _():
            score(0, 0)
            absorb(0, 0, GROUP, held)

        for last, size in ((3, 2), (4, GROUP)):
            if last > most:
                continue

            @pl.when(halves == last)
            def _(size=size):
                score(0, 0)
                score(1, 1, size)
                absorb(0, 0, GROUP, held)
                absorb(1, 1, size)

        return

    pl.when(halves != 1)(keep)
    full, short = halves >> 1, halves & 1

    @pl.when(full > 0)
    def _():
        score(0, 0)

        def two(pair, carry):
            step = 2 * pair
            score(step + 1, 1)
            absorb(step, 0)
            score(step + 2, 0)
            absorb(step + 1, 1)
            return carry

        lax.fori_loop(0, (full - 1) >> 1, two, 0)
        odd = (full & 1) == 1

        @pl.when(odd & (short == 0))
        def _():
            absorb(full - 1, 0)

        @pl.when(odd & (short == 1))
        def _():
            score(full, 1, 2)
            absorb(full - 1, 0)
            absorb(full, 1, 2)

        @pl.when((~odd) & (short == 0))
        def _():
            score(full - 1, 1)
            absorb(full - 2, 0)
            absorb(full - 1, 1)

        @pl.when((~odd) & (short == 1))
        def _():
            score(full - 1, 1)
            absorb(full - 2, 0)
            score(full, 0, 2)
            absorb(full - 1, 1)
            absorb(full, 0, 2)


def result_of(state, head):
    m_ref, acc_ref = state
    rows = slice(head * SPAN, (head + 1) * SPAN)
    weight = acc_ref[rows, HD:]
    live = weight > 0
    safe = jnp.where(live, weight, 1.0)
    value = jnp.where(live, acc_ref[rows, :HD] / safe, 0.0)
    return value, jnp.where(live, m_ref[rows, :] + jnp.log(safe) * math.log2(math.e), NEVER)


STATE, PACKET, RESULT = range(3)


def attend_kernel(u, arrays, begun, gives, table_ref, queries_ref, *refs):
    *refs, list_ref, listed = refs
    fetch = pltpu.make_async_copy(table_ref, list_ref, listed)
    fetch.start()
    kv_refs, refs = refs[:arrays], refs[arrays:]
    held = FRESH
    if begun:
        m_in, acc_in, *refs = refs
        held = (m_in, acc_in)
    if gives == STATE:
        m_ref, acc_ref, *refs = refs
    elif gives == PACKET:
        packet_ref, *refs = refs
    else:
        value_ref, log_ref, *refs = refs
    if begun:
        q_ref = queries_ref
    else:
        q_ref, *refs = refs
        split_queries(queries_ref, q_ref)
    if gives != STATE:
        m_ref, acc_ref, *refs = refs
    if arrays > 1:
        kv_ref, *refs = refs
        at = 0
        for ref in kv_refs:
            kv_ref[at : at + ref.shape[0], :] = ref[...]
            at += ref.shape[0]
    else:
        kv_ref = kv_refs[0]
    s_ref, top_ref = refs
    state = (m_ref, acc_ref)
    most = len(LISTS[u][1]) // 2
    fetch.wait()
    steps_of(list_ref[u, STEPS], most, list_ref, u, kv_ref, q_ref, state, held, s_ref, top_ref)

    if gives == PACKET:
        lane = lax.broadcasted_iota(jnp.int32, (SPAN, HD), 1)
        logs = jnp.zeros((SPAN, HD), jnp.float32)
        for head in range(HEADS):
            value, rest = result_of(state, head)
            packet_ref[head * SPAN : (head + 1) * SPAN, :] = value.astype(jnp.bfloat16)
            for part in range(3):
                piece = rest.astype(jnp.bfloat16).astype(jnp.float32)
                logs = jnp.where(lane == part * HEADS + head, piece, logs)
                rest = rest - piece
        packet_ref[ROWS:, :] = logs.T[: 4 * HEADS, :].astype(jnp.bfloat16)
    elif gives == RESULT:
        for head in range(HEADS):
            rows = slice(head * SPAN, (head + 1) * SPAN)
            value_ref[rows, :], log_ref[rows, :] = result_of(state, head)


def attend(u, gives, table, queries, arrays, state=()):
    count = len(LISTS[u][1])
    maxima = jax.ShapeDtypeStruct((ROWS, HD), jnp.float32)
    sums = jax.ShapeDtypeStruct((ROWS, 2 * HD), jnp.float32)
    split = jax.ShapeDtypeStruct((ROWS, 2 * HD), jnp.bfloat16)
    out = {
        STATE: [maxima, sums],
        PACKET: [jax.ShapeDtypeStruct((ROWS + 4 * HEADS, HD), jnp.bfloat16)],
        RESULT: [maxima, maxima],
    }[gives]
    scratch = []
    if not state:
        if gives == STATE:
            out = [*out, split]
        else:
            scratch.append(VMEM(split.shape, split.dtype))
    if gives != STATE:
        scratch += [VMEM(maxima.shape, maxima.dtype), VMEM(sums.shape, sums.dtype)]
    if len(arrays) > 1:
        scratch.append(VMEM((count * SPAN, 2 * HD), jnp.bfloat16))
    scratch += [VMEM((2, ROWS, BLOCK), jnp.float32), VMEM((2, ROWS, HD), jnp.float32)]
    scratch += [pltpu.SMEM((TABLE, STEPS + 1), jnp.int32), pltpu.SemaphoreType.DMA]
    return pl.pallas_call(
        functools.partial(attend_kernel, u, len(arrays), len(state) > 0, gives),
        out_shape=out,
        in_specs=[whole()] * (2 + len(arrays) + len(state)),
        out_specs=[whole()] * len(out),
        scratch_shapes=scratch,
        compiler_params=limit(24),
        cost_estimate=cost(4 * count * ROWS * SPAN * HD, count * SPAN * SPAN * 4, count * ROWS * SPAN),
    )(table, queries, *arrays, *state)


def merge_kernel(value_ref, log_ref, beside_ref, out_ref, block_ref, done):
    parts = beside_ref[ROWS:, :].astype(jnp.float32)
    logs = parts[:HEADS, :] + parts[HEADS : 2 * HEADS, :] + parts[2 * HEADS : 3 * HEADS, :]
    logs = jnp.concatenate([logs] * (HD // HEADS), axis=0).T
    copies = []
    for head in range(HEADS):
        rows = slice(head * SPAN, (head + 1) * SPAN)
        columns = slice(head * HD, (head + 1) * HD)
        near = log_ref[rows, :]
        far = jnp.broadcast_to(logs[:, head : head + 1], (SPAN, HD))
        top = jnp.maximum(near, far)
        near, far = jnp.exp2(near - top), jnp.exp2(far - top)
        value = value_ref[rows, :] * near + beside_ref[rows, :].astype(jnp.float32) * far
        block_ref[head] = value / (near + far)
        copies.append(pltpu.make_async_copy(block_ref.at[head], out_ref.at[:, columns], done.at[head]))
        copies[-1].start()
    for copy in copies:
        copy.wait()


def merged(value, log, beside):
    return pl.pallas_call(
        merge_kernel,
        out_shape=jax.ShapeDtypeStruct((SPAN, HEADS * HD), jnp.float32),
        in_specs=[whole()] * 3,
        out_specs=whole(pltpu.HBM),
        scratch_shapes=[VMEM((HEADS, SPAN, HD), jnp.float32), pltpu.SemaphoreType.DMA((HEADS,))],
        compiler_params=limit(8),
        name="merge",
        cost_estimate=cost(8 * ROWS * HD, 16 * ROWS * HD, 2 * ROWS * HD),
    )(value, log, beside)


def together(keys, values):
    first = lax.broadcasted_iota(jnp.int32, (SPAN, 2 * HD), 1) < HD
    return jnp.where(first, jnp.pad(keys, ((0, 0), (0, HD))), jnp.pad(values, ((0, 0), (HD, 0))))


def attention(queries, keys, values, span_order):
    beside = send(queries, ACROSS_Y)
    kv = together(keys, values)
    by_a, by_b, also_b = {}, {}, {}
    for d in (2, -1, 1):
        by_a[d] = send(kv, along_a(-d))
    table = lists(span_order)
    plane = jnp.concatenate([kv, *(by_a[d] for d in NEAR_A[1:])], axis=0)
    also_plane = send(plane, ACROSS_CORE)
    for d in (2, -1, 1):
        by_b[d] = send(plane, along_b(-d))
        also_b[d] = send(by_b[d], ACROSS_CORE)
    *state, split = attend(0, STATE, table, beside, [plane, also_plane])
    state = attend(1, STATE, table, split, [by_b[2]], state)
    state = attend(2, STATE, table, split, [also_b[2], by_b[-1], by_b[1]], state)
    (packet,) = attend(3, PACKET, table, split, [also_b[-1], also_b[1]], state)
    back = send(packet, ACROSS_Y)
    arrays = [plane, also_plane, by_b[2], also_b[2], by_b[-1], by_b[1], also_b[-1], also_b[1]]
    value, log = attend(4, RESULT, table, queries, arrays)
    return merged(value, log, back)


def solution(mesh):
    placed = (P(("row", "col"), "grp"), P(("col", "row"), "grp"), P(("col", "row"), "grp"), P())
    return jax.shard_map(
        attention, mesh=mesh, in_specs=placed, out_specs=P(("row", "col"), "grp"), check_vma=False
    )
```

profile of v0, /device:TPU:23, one launch (start us, length us, event | category | flops | bytes accessed | tf_op | source)
XLA Modules:
  0.0 43.8 jit_solution(2947496081343502999)
XLA Ops:
  0.0 0.8 %pad_select_fusion = bf16[128,256]{1,0:T(8,128)(2,1)S(1)} fusion(bf16[128,128]{1,0:T(8,128)(2,1)} %param.6, bf16[128,128]{1,0:T(8,128)(2,1)} %param.5, pred[256]{0:T(512)(128)(4,1)S(1)} %iota_compare_fusion), kind=kLoop, calls=%fused_computation.1 | loop fusion | flops 32768 | bytes 131328 | tf_op jit(solution)/shard_map/jit(_where)/select_n | solution.py:402
  0.8 0.0 copy-start.1
  0.8 0.0 copy-start
  0.8 0.3 collective-permute-start
  1.1 1.3 %collective-permute-start.1 = (bf16[128,256]{1,0:T(8,128)(2,1)S(1)}, bf16[128,256]{1,0:T(8,128)(2,1)S(1)}, u32[]{:S(2)}, u32[]{:S(2)}) collective-permute-start(bf16[128,256]{1,0:T(8,128)(2,1)S(1)} %pad_select_fusion), channel_id=1, source_target_pairs={{0,48},{1,7},{2,50},{3,1},{4,52},{5,3},{6,54},{7,5},{8,56},{9,15},... | collective-permute-start | bytes 196616 | tf_op jit(solution)/shard_map/ppermute | solution.py:51
  2.4 1.1 %collective-permute-start.2 = (bf16[128,256]{1,0:T(8,128)(2,1)S(1)}, bf16[128,256]{1,0:T(8,128)(2,1)S(1)}, u32[]{:S(2)}, u32[]{:S(2)}) collective-permute-start(bf16[128,256]{1,0:T(8,128)(2,1)S(1)} %pad_select_fusion), channel_id=1, source_target_pairs={{0,32},{1,5},{2,34},{3,7},{4,36},{5,1},{6,38},{7,3},{8,40},{9,13},... | collective-permute-start | bytes 196616 | tf_op jit(solution)/shard_map/ppermute | solution.py:51
  3.5 0.5 %collective-permute-done = bf16[128,256]{1,0:T(8,128)(2,1)S(1)} collective-permute-done((bf16[128,256]{1,0:T(8,128)(2,1)S(1)}, bf16[128,256]{1,0:T(8,128)(2,1)S(1)}, u32[]{:S(2)}, u32[]{:S(2)}) %collective-permute-start) | collective-permute-done | bytes 65568 | tf_op jit(solution)/shard_map/ppermute | solution.py:51
  4.0 1.4 %collective-permute-done.1 = bf16[128,256]{1,0:T(8,128)(2,1)S(1)} collective-permute-done((bf16[128,256]{1,0:T(8,128)(2,1)S(1)}, bf16[128,256]{1,0:T(8,128)(2,1)S(1)}, u32[]{:S(2)}, u32[]{:S(2)}) %collective-permute-start.1) | collective-permute-done | bytes 65568 | tf_op jit(solution)/shard_map/ppermute | solution.py:51
  5.4 1.6 %collective-permute-done.2 = bf16[128,256]{1,0:T(8,128)(2,1)S(1)} collective-permute-done((bf16[128,256]{1,0:T(8,128)(2,1)S(1)}, bf16[128,256]{1,0:T(8,128)(2,1)S(1)}, u32[]{:S(2)}, u32[]{:S(2)}) %collective-permute-start.2) | collective-permute-done | bytes 65568 | tf_op jit(solution)/shard_map/ppermute | solution.py:51
  7.0 3.7 %collective-permute-start.4 = (bf16[512,256]{1,0:T(8,128)(2,1)S(1)}, bf16[512,256]{1,0:T(8,128)(2,1)S(1)}, u32[]{:S(2)}, u32[]{:S(2)}) collective-permute-start(bf16[512,256]{1,0:T(8,128)(2,1)S(1)} %pad_maximum_fusion.refs_0_), channel_id=1, source_target_pairs={{0,4},{1,33},{2,6},{3,35},{4,0},{5,37},{6,2},{7,39},{8,12},{9,41},... | collective-permute-start | bytes 786440 | tf_op jit(solution)/shard_map/ppermute | solution.py:51
  10.7 0.7 %collective-permute-start.6 = (bf16[512,256]{1,0:T(8,128)(2,1)S(1)}, bf16[512,256]{1,0:T(8,128)(2,1)S(1)}, u32[]{:S(2)}, u32[]{:S(2)}) collective-permute-start(bf16[512,256]{1,0:T(8,128)(2,1)S(1)} %pad_maximum_fusion.refs_0_), channel_id=1, source_target_pairs={{0,2},{1,17},{2,4},{3,19},{4,6},{5,21},{6,0},{7,23},{8,10},{9,25},... | collective-permute-start | bytes 786440 | tf_op jit(solution)/shard_map/ppermute | solution.py:51
  11.4 1.9 %collective-permute-start.7 = (bf16[512,256]{1,0:T(8,128)(2,1)S(1)}, bf16[512,256]{1,0:T(8,128)(2,1)S(1)}, u32[]{:S(2)}, u32[]{:S(2)}) collective-permute-start(bf16[512,256]{1,0:T(8,128)(2,1)S(1)} %pad_maximum_fusion.refs_0_), channel_id=1, source_target_pairs={{0,6},{1,49},{2,0},{3,51},{4,2},{5,53},{6,4},{7,55},{8,14},{9,57},... | collective-permute-start | bytes 786440 | tf_op jit(solution)/shard_map/ppermute | solution.py:51
  13.4 0.0 copy-done.1
  13.4 1.0 %collective-permute-start.10 = (bf16[128,1024]{1,0:T(8,128)(2,1)S(1)}, bf16[128,1024]{1,0:T(8,128)(2,1)S(1)}, u32[]{:S(2)}, u32[]{:S(2)}) collective-permute-start(bf16[128,1024]{1,0:T(8,128)(2,1)S(1)} %copy-done.1), channel_id=1, source_target_pairs={{0,8},{1,9},{2,10},{3,11},{4,12},{5,13},{6,14},{7,15},{8,0},{9,1},... | collective-permute-start | bytes 786440 | tf_op jit(solution)/shard_map/ppermute | solution.py:51
  14.4 2.0 %collective-permute-start.3 = (bf16[512,256]{1,0:T(8,128)(2,1)S(1)}, bf16[512,256]{1,0:T(8,128)(2,1)S(1)}, u32[]{:S(2)}, u32[]{:S(2)}) collective-permute-start(bf16[512,256]{1,0:T(8,128)(2,1)S(1)} %pad_maximum_fusion.refs_0_), channel_id=1, source_target_pairs={{0,1},{1,0},{2,3},{3,2},{4,5},{5,4},{6,7},{7,6},{8,9},{9,8},{10,11... | collective-permute-start | bytes 786440 | tf_op jit(solution)/shard_map/ppermute | solution.py:51
  16.4 0.0 collective-permute-done.4.refs_2_.refs_0_
  16.4 3.1 %collective-permute-start.5 = (bf16[512,256]{1,0:T(8,128)(2,1)S(1)}, bf16[512,256]{1,0:T(8,128)(2,1)S(1)}, u32[]{:S(2)}, u32[]{:S(2)}) collective-permute-start(bf16[512,256]{1,0:T(8,128)(2,1)S(1)} %collective-permute-done.4.refs_2_.refs_0_), channel_id=1, source_target_pairs={{0,1},{1,0},{2,3},{3,2},{4,5},{5,4},{6,7},{7,6},{8,9},{9,8},{10,11... | collective-permute-start | bytes 786440 | tf_op jit(solution)/shard_map/ppermute | solution.py:51
  19.4 0.0 collective-permute-done.6.refs_4_.refs_1_
  19.4 0.6 %collective-permute-start.8 = (bf16[512,256]{1,0:T(8,128)(2,1)S(1)}, bf16[512,256]{1,0:T(8,128)(2,1)S(1)}, u32[]{:S(2)}, u32[]{:S(2)}) collective-permute-start(bf16[512,256]{1,0:T(8,128)(2,1)S(1)} %collective-permute-done.6.refs_4_.refs_1_), channel_id=1, source_target_pairs={{0,1},{1,0},{2,3},{3,2},{4,5},{5,4},{6,7},{7,6},{8,9},{9,8},{10,11... | collective-permute-start | bytes 786440 | tf_op jit(solution)/shard_map/ppermute | solution.py:51
  20.0 0.0 collective-permute-done.7.refs_5_.refs_2_
  20.1 2.6 %collective-permute-start.9 = (bf16[512,256]{1,0:T(8,128)(2,1)S(1)}, bf16[512,256]{1,0:T(8,128)(2,1)S(1)}, u32[]{:S(2)}, u32[]{:S(2)}) collective-permute-start(bf16[512,256]{1,0:T(8,128)(2,1)S(1)} %collective-permute-done.7.refs_5_.refs_2_), channel_id=1, source_target_pairs={{0,1},{1,0},{2,3},{3,2},{4,5},{5,4},{6,7},{7,6},{8,9},{9,8},{10,11... | collective-permute-start | bytes 786440 | tf_op jit(solution)/shard_map/ppermute | solution.py:51
  22.6 0.0 copy-done
  22.6 1.7 %lists.1.table_ref = s32[8,128]{1,0:T(8,128)S(1)} custom-call(s32[64]{0:T(128)S(1)} %copy-done), custom_call_target="tpu_custom_call" | custom-call | flops 1024 | bytes 1024 | tf_op jit(solution)/shard_map/lists/pallas_call | solution.py:116
  24.3 0.0 collective-permute-done.10.queries_ref
  24.4 0.0 collective-permute-done.3.refs_1_
  24.4 1.8 %shard_map.47 = (f32[1024,128]{1,0:T(8,128)S(1)}, f32[1024,256]{1,0:T(8,128)S(1)}, bf16[1024,256]{1,0:T(8,128)(2,1)S(1)}) custom-call(s32[8,128]{1,0:T(8,128)S(1)} %lists.1.table_ref, bf16[128,1024]{1,0:T(8,128)(2,1)S(1)} %collective-permute-done.10.queries_ref, bf16[512,256]{1,0:T(8,128)(2,1)S(1)} %pad_maximum_fusion.refs_0_, ...), custom_call_target="tpu_custom_call" | custom-call | flops 536870912 | bytes 524288 | tf_op jit(solution)/shard_map/pallas_call | solution.py:356
  26.2 1.9 %shard_map.48 = (f32[1024,128]{1,0:T(8,128)S(1)}, f32[1024,256]{1,0:T(8,128)S(1)}) custom-call(s32[8,128]{1,0:T(8,128)S(1)} %lists.1.table_ref, bf16[1024,256]{1,0:T(8,128)(2,1)S(1)} %get-tuple-element.16.queries_ref, bf16[512,256]{1,0:T(8,128)(2,1)S(1)} %collective-permute-done.4.refs_2_.refs_0_, f32[1024,128]{1,0:T(8,128)S(1)} %get-tuple-element.17.refs_1_, ...), custom_call_target="tpu_custom_call" | custom-call | flops 268435456 | bytes 262144 | tf_op jit(solution)/shard_map/pallas_call | solution.py:356
  28.1 0.0 collective-permute-done.5.refs_3_.refs_0_
  28.1 3.3 %shard_map.49 = (f32[1024,128]{1,0:T(8,128)S(1)}, f32[1024,256]{1,0:T(8,128)S(1)}) custom-call(s32[8,128]{1,0:T(8,128)S(1)} %lists.1.table_ref, bf16[1024,256]{1,0:T(8,128)(2,1)S(1)} %get-tuple-element.16.queries_ref, bf16[512,256]{1,0:T(8,128)(2,1)S(1)} %collective-permute-done.5.refs_3_.refs_0_, ...), custom_call_target="tpu_custom_call" | custom-call | flops 805306368 | bytes 786432 | tf_op jit(solution)/shard_map/pallas_call | solution.py:356
  31.4 0.0 collective-permute-done.8.refs_6_.refs_0_
  31.4 0.0 collective-permute-done.9.refs_7_.refs_1_
  31.4 2.7 %shard_map.50 = bf16[1056,128]{1,0:T(8,128)(2,1)S(1)} custom-call(s32[8,128]{1,0:T(8,128)S(1)} %lists.1.table_ref, bf16[1024,256]{1,0:T(8,128)(2,1)S(1)} %get-tuple-element.16.queries_ref, bf16[512,256]{1,0:T(8,128)(2,1)S(1)} %collective-permute-done.8.refs_6_.refs_0_, bf16[512,256]{1,0:T(8,128)(2,1)S(1)} %collective-permute-done.9.refs_7_.refs_1_, ...), custom_call_target="tpu_custom_call" | custom-call | flops 536870912 | bytes 524288 | tf_op jit(solution)/shard_map/pallas_call | solution.py:356
  34.1 0.1 collective-permute-start.11
  34.2 3.4 %shard_map.46 = (f32[1024,128]{1,0:T(8,128)S(1)}, f32[1024,128]{1,0:T(8,128)S(1)}) custom-call(s32[8,128]{1,0:T(8,128)S(1)} %lists.1.table_ref, bf16[128,1024]{1,0:T(8,128)(2,1)S(1)} %copy-done.1, bf16[512,256]{1,0:T(8,128)(2,1)S(1)} %pad_maximum_fusion.refs_0_, bf16[512,256]{1,0:T(8,128)(2,1)S(1)} %collective-permute-done.3.refs_1_, ...), custom_call_target="tpu_custom_call" | custom-call | flops 2147483648 | bytes 2097152 | tf_op jit(solution)/shard_map/pallas_call | solution.py:356
  37.5 4.9 %collective-permute-done.11.beside_ref = bf16[1056,128]{1,0:T(8,128)(2,1)S(1)} collective-permute-done((bf16[1056,128]{1,0:T(8,128)(2,1)S(1)}, bf16[1056,128]{1,0:T(8,128)(2,1)S(1)}, u32[]{:S(2)}, u32[]{:S(2)}) %collective-permute-start.11) | collective-permute-done | bytes 270368 | tf_op jit(solution)/shard_map/ppermute | solution.py:51
  42.4 1.2 %merge.1 = f32[128,1024]{1,0:T(8,128)} custom-call(f32[1024,128]{1,0:T(8,128)S(1)} %get-tuple-element.14.value_ref, f32[1024,128]{1,0:T(8,128)S(1)} %get-tuple-element.15.log_ref, bf16[1056,128]{1,0:T(8,128)(2,1)S(1)} %collective-permute-done.11.beside_ref), custom_call_target="tpu_custom_call" | custom-call | flops 1048576 | bytes 2097152 | tf_op jit(solution)/shard_map/merge/pallas_call | solution.py:388
  (2 shorter events, 0.0 us)
Async XLA Ops:
  0.8 12.6 %copy-start.1 = (bf16[128,1024]{1,0:T(8,128)(2,1)S(1)}, bf16[128,1024]{1,0:T(8,128)(2,1)}, u32[]{:S(2)}) copy-start(bf16[128,1024]{1,0:T(8,128)(2,1)} %queries_ref.1) | copy-start | bytes 786436
  0.8 21.8 %copy-start = (s32[64]{0:T(128)S(1)}, s32[64]{0:T(128)}, u32[]{:S(2)}) copy-start(s32[64]{0:T(128)} %order_ref.1) | copy-start | bytes 772
  0.8 3.2 %collective-permute-start = (bf16[128,256]{1,0:T(8,128)(2,1)S(1)}, bf16[128,256]{1,0:T(8,128)(2,1)S(1)}, u32[]{:S(2)}, u32[]{:S(2)}) collective-permute-start(bf16[128,256]{1,0:T(8,128)(2,1)S(1)} %pad_select_fusion), channel_id=1, source_target_pairs={{0,16},{1,3},{2,18},{3,5},{4,20},{5,7},{6,22},{7,1},{8,24},{9,11},... | collective-permute-start | bytes 196616 | tf_op jit(solution)/shard_map/ppermute | solution.py:51
  1.1 4.3 %collective-permute-start.1 = (bf16[128,256]{1,0:T(8,128)(2,1)S(1)}, bf16[128,256]{1,0:T(8,128)(2,1)S(1)}, u32[]{:S(2)}, u32[]{:S(2)}) collective-permute-start(bf16[128,256]{1,0:T(8,128)(2,1)S(1)} %pad_select_fusion), channel_id=1, source_target_pairs={{0,48},{1,7},{2,50},{3,1},{4,52},{5,3},{6,54},{7,5},{8,56},{9,15},... | collective-permute-start | bytes 196616 | tf_op jit(solution)/shard_map/ppermute | solution.py:51
  2.4 4.6 %collective-permute-start.2 = (bf16[128,256]{1,0:T(8,128)(2,1)S(1)}, bf16[128,256]{1,0:T(8,128)(2,1)S(1)}, u32[]{:S(2)}, u32[]{:S(2)}) collective-permute-start(bf16[128,256]{1,0:T(8,128)(2,1)S(1)} %pad_select_fusion), channel_id=1, source_target_pairs={{0,32},{1,5},{2,34},{3,7},{4,36},{5,1},{6,38},{7,3},{8,40},{9,13},... | collective-permute-start | bytes 196616 | tf_op jit(solution)/shard_map/ppermute | solution.py:51
  7.0 9.4 %collective-permute-start.4 = (bf16[512,256]{1,0:T(8,128)(2,1)S(1)}, bf16[512,256]{1,0:T(8,128)(2,1)S(1)}, u32[]{:S(2)}, u32[]{:S(2)}) collective-permute-start(bf16[512,256]{1,0:T(8,128)(2,1)S(1)} %pad_maximum_fusion.refs_0_), channel_id=1, source_target_pairs={{0,4},{1,33},{2,6},{3,35},{4,0},{5,37},{6,2},{7,39},{8,12},{9,41},... | collective-permute-start | bytes 786440 | tf_op jit(solution)/shard_map/ppermute | solution.py:51
  10.7 8.8 %collective-permute-start.6 = (bf16[512,256]{1,0:T(8,128)(2,1)S(1)}, bf16[512,256]{1,0:T(8,128)(2,1)S(1)}, u32[]{:S(2)}, u32[]{:S(2)}) collective-permute-start(bf16[512,256]{1,0:T(8,128)(2,1)S(1)} %pad_maximum_fusion.refs_0_), channel_id=1, source_target_pairs={{0,2},{1,17},{2,4},{3,19},{4,6},{5,21},{6,0},{7,23},{8,10},{9,25},... | collective-permute-start | bytes 786440 | tf_op jit(solution)/shard_map/ppermute | solution.py:51
  11.4 8.6 %collective-permute-start.7 = (bf16[512,256]{1,0:T(8,128)(2,1)S(1)}, bf16[512,256]{1,0:T(8,128)(2,1)S(1)}, u32[]{:S(2)}, u32[]{:S(2)}) collective-permute-start(bf16[512,256]{1,0:T(8,128)(2,1)S(1)} %pad_maximum_fusion.refs_0_), channel_id=1, source_target_pairs={{0,6},{1,49},{2,0},{3,51},{4,2},{5,53},{6,4},{7,55},{8,14},{9,57},... | collective-permute-start | bytes 786440 | tf_op jit(solution)/shard_map/ppermute | solution.py:51
  13.4 11.0 %collective-permute-start.10 = (bf16[128,1024]{1,0:T(8,128)(2,1)S(1)}, bf16[128,1024]{1,0:T(8,128)(2,1)S(1)}, u32[]{:S(2)}, u32[]{:S(2)}) collective-permute-start(bf16[128,1024]{1,0:T(8,128)(2,1)S(1)} %copy-done.1), channel_id=1, source_target_pairs={{0,8},{1,9},{2,10},{3,11},{4,12},{5,13},{6,14},{7,15},{8,0},{9,1},... | collective-permute-start | bytes 786440 | tf_op jit(solution)/shard_map/ppermute | solution.py:51
  14.4 10.0 %collective-permute-start.3 = (bf16[512,256]{1,0:T(8,128)(2,1)S(1)}, bf16[512,256]{1,0:T(8,128)(2,1)S(1)}, u32[]{:S(2)}, u32[]{:S(2)}) collective-permute-start(bf16[512,256]{1,0:T(8,128)(2,1)S(1)} %pad_maximum_fusion.refs_0_), channel_id=1, source_target_pairs={{0,1},{1,0},{2,3},{3,2},{4,5},{5,4},{6,7},{7,6},{8,9},{9,8},{10,11... | collective-permute-start | bytes 786440 | tf_op jit(solution)/shard_map/ppermute | solution.py:51
  16.4 11.7 %collective-permute-start.5 = (bf16[512,256]{1,0:T(8,128)(2,1)S(1)}, bf16[512,256]{1,0:T(8,128)(2,1)S(1)}, u32[]{:S(2)}, u32[]{:S(2)}) collective-permute-start(bf16[512,256]{1,0:T(8,128)(2,1)S(1)} %collective-permute-done.4.refs_2_.refs_0_), channel_id=1, source_target_pairs={{0,1},{1,0},{2,3},{3,2},{4,5},{5,4},{6,7},{7,6},{8,9},{9,8},{10,11... | collective-permute-start | bytes 786440 | tf_op jit(solution)/shard_map/ppermute | solution.py:51
  19.4 11.9 %collective-permute-start.8 = (bf16[512,256]{1,0:T(8,128)(2,1)S(1)}, bf16[512,256]{1,0:T(8,128)(2,1)S(1)}, u32[]{:S(2)}, u32[]{:S(2)}) collective-permute-start(bf16[512,256]{1,0:T(8,128)(2,1)S(1)} %collective-permute-done.6.refs_4_.refs_1_), channel_id=1, source_target_pairs={{0,1},{1,0},{2,3},{3,2},{4,5},{5,4},{6,7},{7,6},{8,9},{9,8},{10,11... | collective-permute-start | bytes 786440 | tf_op jit(solution)/shard_map/ppermute | solution.py:51
  20.1 11.3 %collective-permute-start.9 = (bf16[512,256]{1,0:T(8,128)(2,1)S(1)}, bf16[512,256]{1,0:T(8,128)(2,1)S(1)}, u32[]{:S(2)}, u32[]{:S(2)}) collective-permute-start(bf16[512,256]{1,0:T(8,128)(2,1)S(1)} %collective-permute-done.7.refs_5_.refs_2_), channel_id=1, source_target_pairs={{0,1},{1,0},{2,3},{3,2},{4,5},{5,4},{6,7},{7,6},{8,9},{9,8},{10,11... | collective-permute-start | bytes 786440 | tf_op jit(solution)/shard_map/ppermute | solution.py:51
  34.1 8.4 %collective-permute-start.11 = (bf16[1056,128]{1,0:T(8,128)(2,1)S(1)}, bf16[1056,128]{1,0:T(8,128)(2,1)S(1)}, u32[]{:S(2)}, u32[]{:S(2)}) collective-permute-start(bf16[1056,128]{1,0:T(8,128)(2,1)S(1)} %shard_map.50), channel_id=1, source_target_pairs={{0,8},{1,9},{2,10},{3,11},{4,12},{5,13},{6,14},{7,15},{8,0},{9,1},... | collective-permute-start | bytes 811016 | tf_op jit(solution)/shard_map/ppermute | solution.py:51
where the time goes:
time: 44 us; the launch traced here: 43.8 us
  starting transfers between devices  18.4 us (42%)
  Pallas kernels  15.9 us (36%)
  waiting for transfers between devices  8.44 us (19%)
  other arithmetic  0.81 us (2%)
    ppermute x12, starting transfers between devices, send(): return lax.ppermute(x, AXES, perm)  18.4 us
    pallas_call x5, Pallas kernels, attend(): pl.pallas_call(functools.partial(attend_kernel, u, len(arrays), len(state...  13 us
    ppermute x12, waiting for transfers between devices, send(): return lax.ppermute(x, AXES, perm)  8.44 us
    pallas_call x1, Pallas kernels, lists(): pl.pallas_call(lists_kernel, out_shape=jax.ShapeDtypeStruct((TABLE, STEPS...  1.69 us
    pallas_call x1, Pallas kernels, merged(): pl.pallas_call(merge_kernel, out_shape=jax.ShapeDtypeStruct((SPAN, HEADS...  1.18 us
  transfers between devices with their start and end apart: 12, of which 4 were waited for; matrix products, arithmetic and copies ran while one was open for 0% of the time, Pallas kernels for 27%

commit v1 on v0

--- a/solution.py
+++ b/solution.py
@@ -201,24 +201,18 @@
         score(0, 0, 2)
         absorb(0, 0, 2, held)
 
-    if most <= 4:
+    if most <= 6:
         pl.when(halves == 0)(keep)
-
-        @pl.when(halves == 2)
-        def _():
-            score(0, 0)
-            absorb(0, 0, GROUP, held)
-
-        for last, size in ((3, 2), (4, GROUP)):
-            if last > most:
-                continue
+        for last in range(2, most + 1):
+            sizes = [GROUP] * (last // 2) + [2] * (last % 2)
 
             @pl.when(halves == last)
-            def _(size=size):
-                score(0, 0)
-                score(1, 1, size)
-                absorb(0, 0, GROUP, held)
-                absorb(1, 1, size)
+            def _(sizes=sizes):
+                score(0, 0, sizes[0])
+                for step, size in enumerate(sizes):
+                    if step + 1 < len(sizes):
+                        score(step + 1, (step + 1) % 2, sizes[step + 1])
+                    absorb(step, step % 2, size, held if step == 0 else None)
 
         return
 
@@ -265,14 +259,22 @@
             absorb(full, 0, 2)
 
 
-def result_of(state, head):
+def in_lanes(columns):
+    lane = lax.broadcasted_iota(jnp.int32, (SPAN, HD), 1)
+    out = jnp.zeros((SPAN, HD), jnp.float32)
+    for head, column in enumerate(columns):
+        out = jnp.where(lane == head, column, out)
+    return out
+
+
+def statistics(state):
     m_ref, acc_ref = state
-    rows = slice(head * SPAN, (head + 1) * SPAN)
-    weight = acc_ref[rows, HD:]
-    live = weight > 0
-    safe = jnp.where(live, weight, 1.0)
-    value = jnp.where(live, acc_ref[rows, :HD] / safe, 0.0)
-    return value, jnp.where(live, m_ref[rows, :] + jnp.log(safe) * math.log2(math.e), NEVER)
+    rows = [slice(head * SPAN, (head + 1) * SPAN) for head in range(HEADS)]
+    return in_lanes([m_ref[r, :] for r in rows]), in_lanes([acc_ref[r, HD:] for r in rows])
+
+
+def along_lanes(columns, head):
+    return jnp.broadcast_to(columns[:, head : head + 1], (SPAN, HD))
 
 
 STATE, PACKET, RESULT = range(3)
@@ -292,7 +294,7 @@
     elif gives == PACKET:
         packet_ref, *refs = refs
     else:
-        value_ref, log_ref, *refs = refs
+        sums_ref, stats_ref, *refs = refs
     if begun:
         q_ref = queries_ref
     else:
@@ -315,20 +317,27 @@
     steps_of(list_ref[u, STEPS], most, list_ref, u, kv_ref, q_ref, state, held, s_ref, top_ref)
 
     if gives == PACKET:
+        top, weight = statistics(state)
+        live = weight > 0
+        safe = jnp.where(live, weight, 1.0)
+        inverse = jnp.where(live, 1.0 / safe, 0.0)
+        rest = jnp.where(live, top + jnp.log(safe) * math.log2(math.e), NEVER)
         lane = lax.broadcasted_iota(jnp.int32, (SPAN, HD), 1)
+        rest = jnp.where(lane < HEADS, rest, 0.0)
         logs = jnp.zeros((SPAN, HD), jnp.float32)
-        for head in range(HEADS):
-            value, rest = result_of(state, head)
-            packet_ref[head * SPAN : (head + 1) * SPAN, :] = value.astype(jnp.bfloat16)
-            for part in range(3):
-                piece = rest.astype(jnp.bfloat16).astype(jnp.float32)
-                logs = jnp.where(lane == part * HEADS + head, piece, logs)
-                rest = rest - piece
+        for part in range(3):
+            piece = rest.astype(jnp.bfloat16).astype(jnp.float32)
+            logs = logs + (pltpu.roll(piece, part * HEADS, 1) if part else piece)
+            rest = rest - piece
         packet_ref[ROWS:, :] = logs.T[: 4 * HEADS, :].astype(jnp.bfloat16)
-    elif gives == RESULT:
         for head in range(HEADS):
             rows = slice(head * SPAN, (head + 1) * SPAN)
-            value_ref[rows, :], log_ref[rows, :] = result_of(state, head)
+            packet_ref[rows, :] = (acc_ref[rows, :HD] * along_lanes(inverse, head)).astype(jnp.bfloat16)
+    elif gives == RESULT:
+        top, weight = statistics(state)
+        lane = lax.broadcasted_iota(jnp.int32, (SPAN, HD), 1)
+        stats_ref[...] = jnp.where(lane < HEADS, top, pltpu.roll(weight, HEADS, 1))
+        sums_ref[...] = acc_ref[:, :HD]
 
 
 def attend(u, gives, table, queries, arrays, state=()):
@@ -339,7 +348,7 @@
     out = {
         STATE: [maxima, sums],
         PACKET: [jax.ShapeDtypeStruct((ROWS + 4 * HEADS, HD), jnp.bfloat16)],
-        RESULT: [maxima, maxima],
+        RESULT: [maxima, jax.ShapeDtypeStruct((SPAN, HD), jnp.float32)],
     }[gives]
     scratch = []
     if not state:
@@ -364,27 +373,29 @@
     )(table, queries, *arrays, *state)
 
 
-def merge_kernel(value_ref, log_ref, beside_ref, out_ref, block_ref, done):
+def merge_kernel(sums_ref, stats_ref, beside_ref, out_ref, block_ref, done):
     parts = beside_ref[ROWS:, :].astype(jnp.float32)
-    logs = parts[:HEADS, :] + parts[HEADS : 2 * HEADS, :] + parts[2 * HEADS : 3 * HEADS, :]
-    logs = jnp.concatenate([logs] * (HD // HEADS), axis=0).T
+    far = parts[:HEADS, :] + parts[HEADS : 2 * HEADS, :] + parts[2 * HEADS : 3 * HEADS, :]
+    far = jnp.concatenate([far] * (HD // HEADS), axis=0).T
+    near = stats_ref[...]
+    total = pltpu.roll(near, HD - HEADS, 1)
+    top = jnp.maximum(near, far)
+    near, far = jnp.exp2(near - top), jnp.exp2(far - top)
+    total = total * near + far
+    near, far = near / total, far / total
     copies = []
     for head in range(HEADS):
         rows = slice(head * SPAN, (head + 1) * SPAN)
         columns = slice(head * HD, (head + 1) * HD)
-        near = log_ref[rows, :]
-        far = jnp.broadcast_to(logs[:, head : head + 1], (SPAN, HD))
-        top = jnp.maximum(near, far)
-        near, far = jnp.exp2(near - top), jnp.exp2(far - top)
-        value = value_ref[rows, :] * near + beside_ref[rows, :].astype(jnp.float32) * far
-        block_ref[head] = value / (near + far)
+        value = sums_ref[rows, :] * along_lanes(near, head)
+        block_ref[head] = value + beside_ref[rows, :].astype(jnp.float32) * along_lanes(far, head)
         copies.append(pltpu.make_async_copy(block_ref.at[head], out_ref.at[:, columns], done.at[head]))
         copies[-1].start()
     for copy in copies:
         copy.wait()
 
 
-def merged(value, log, beside):
+def merged(sums, stats, beside):
     return pl.pallas_call(
         merge_kernel,
         out_shape=jax.ShapeDtypeStruct((SPAN, HEADS * HD), jnp.float32),
@@ -394,7 +405,7 @@
         compiler_params=limit(8),
         name="merge",
         cost_estimate=cost(8 * ROWS * HD, 16 * ROWS * HD, 2 * ROWS * HD),
-    )(value, log, beside)
+    )(sums, stats, beside)
 
 
 def together(keys, values):
@@ -420,12 +431,10 @@
     (packet,) = attend(3, PACKET, table, split, [also_b[-1], also_b[1]], state)
     back = send(packet, ACROSS_Y)
     arrays = [plane, also_plane, by_b[2], also_b[2], by_b[-1], by_b[1], also_b[-1], also_b[1]]
-    value, log = attend(4, RESULT, table, queries, arrays)
-    return merged(value, log, back)
+    sums, stats = attend(4, RESULT, table, queries, arrays)
+    return merged(sums, stats, back)
 
 
 def solution(mesh):
     placed = (P(("row", "col"), "grp"), P(("col", "row"), "grp"), P(("col", "row"), "grp"), P())
-    return jax.shard_map(
-        attention, mesh=mesh, in_specs=placed, out_specs=P(("row", "col"), "grp"), check_vma=False
-    )
+    return jax.shard_map(attention, mesh=mesh, in_specs=placed, out_specs=P(("row", "col"), "grp"), check_vma=False)

time: 44 us -> 43.4 us (0.986)
  Pallas kernels: 15.9 us -> 15.4 us
    pallas_call x5, Pallas kernels: 13 us -> 12.5 us  [attend(): pl.pallas_call(functools.partial(attend_kernel, u, len(arrays), len(state...]
  transfers between devices with their start and end apart: 12 -> 12, of which waited for: 4 -> 4; matrix products, arithmetic and copies ran while one was open for 0% -> 0% of each run, Pallas kernels for 27% -> 26%
where the time goes in v1:
time: 43.4 us; the launch traced here: 43.3 us
  starting transfers between devices  18.4 us (42%)
  Pallas kernels  15.4 us (35%)
  waiting for transfers between devices  8.41 us (19%)
  other arithmetic  0.81 us (2%)
    ppermute x12, starting transfers between devices, send(): return lax.ppermute(x, AXES, perm)  18.4 us
    pallas_call x5, Pallas kernels, attend(): pl.pallas_call(functools.partial(attend_kernel, u, len(arrays), len(state...  12.5 us
    ppermute x12, waiting for transfers between devices, send(): return lax.ppermute(x, AXES, perm)  8.41 us
    pallas_call x1, Pallas kernels, lists(): pl.pallas_call(lists_kernel, out_shape=jax.ShapeDtypeStruct((TABLE, STEPS...  1.69 us
    pallas_call x1, Pallas kernels, merged(): pl.pallas_call(merge_kernel, out_shape=jax.ShapeDtypeStruct((SPAN, HEADS...  1.16 us
  transfers between devices with their start and end apart: 12, of which 4 were waited for; matrix products, arithmetic and copies ran while one was open for 0% of the time, Pallas kernels for 26%

profile of v1, /device:TPU:23, one launch (start us, length us, event | category | flops | bytes accessed | tf_op | source)
XLA Modules:
  0.0 43.3 jit_solution(5901395995500577842)
XLA Ops:
  0.0 0.8 %pad_select_fusion = bf16[128,256]{1,0:T(8,128)(2,1)S(1)} fusion(bf16[128,128]{1,0:T(8,128)(2,1)} %param.6, bf16[128,128]{1,0:T(8,128)(2,1)} %param.5, pred[256]{0:T(512)(128)(4,1)S(1)} %iota_compare_fusion), kind=kLoop, calls=%fused_computation.1 | loop fusion | flops 32768 | bytes 131328 | tf_op jit(solution)/shard_map/jit(_where)/select_n | solution.py:413
  0.8 0.0 copy-start.1
  0.8 0.0 copy-start
  0.8 0.3 collective-permute-start
  1.1 1.3 %collective-permute-start.1 = (bf16[128,256]{1,0:T(8,128)(2,1)S(1)}, bf16[128,256]{1,0:T(8,128)(2,1)S(1)}, u32[]{:S(2)}, u32[]{:S(2)}) collective-permute-start(bf16[128,256]{1,0:T(8,128)(2,1)S(1)} %pad_select_fusion), channel_id=1, source_target_pairs={{0,48},{1,7},{2,50},{3,1},{4,52},{5,3},{6,54},{7,5},{8,56},{9,15},... | collective-permute-start | bytes 196616 | tf_op jit(solution)/shard_map/ppermute | solution.py:51
  2.4 1.1 %collective-permute-start.2 = (bf16[128,256]{1,0:T(8,128)(2,1)S(1)}, bf16[128,256]{1,0:T(8,128)(2,1)S(1)}, u32[]{:S(2)}, u32[]{:S(2)}) collective-permute-start(bf16[128,256]{1,0:T(8,128)(2,1)S(1)} %pad_select_fusion), channel_id=1, source_target_pairs={{0,32},{1,5},{2,34},{3,7},{4,36},{5,1},{6,38},{7,3},{8,40},{9,13},... | collective-permute-start | bytes 196616 | tf_op jit(solution)/shard_map/ppermute | solution.py:51
  3.5 0.5 %collective-permute-done = bf16[128,256]{1,0:T(8,128)(2,1)S(1)} collective-permute-done((bf16[128,256]{1,0:T(8,128)(2,1)S(1)}, bf16[128,256]{1,0:T(8,128)(2,1)S(1)}, u32[]{:S(2)}, u32[]{:S(2)}) %collective-permute-start) | collective-permute-done | bytes 65568 | tf_op jit(solution)/shard_map/ppermute | solution.py:51
  4.0 1.4 %collective-permute-done.1 = bf16[128,256]{1,0:T(8,128)(2,1)S(1)} collective-permute-done((bf16[128,256]{1,0:T(8,128)(2,1)S(1)}, bf16[128,256]{1,0:T(8,128)(2,1)S(1)}, u32[]{:S(2)}, u32[]{:S(2)}) %collective-permute-start.1) | collective-permute-done | bytes 65568 | tf_op jit(solution)/shard_map/ppermute | solution.py:51
  5.4 1.6 %collective-permute-done.2 = bf16[128,256]{1,0:T(8,128)(2,1)S(1)} collective-permute-done((bf16[128,256]{1,0:T(8,128)(2,1)S(1)}, bf16[128,256]{1,0:T(8,128)(2,1)S(1)}, u32[]{:S(2)}, u32[]{:S(2)}) %collective-permute-start.2) | collective-permute-done | bytes 65568 | tf_op jit(solution)/shard_map/ppermute | solution.py:51
  7.0 3.7 %collective-permute-start.4 = (bf16[512,256]{1,0:T(8,128)(2,1)S(1)}, bf16[512,256]{1,0:T(8,128)(2,1)S(1)}, u32[]{:S(2)}, u32[]{:S(2)}) collective-permute-start(bf16[512,256]{1,0:T(8,128)(2,1)S(1)} %pad_maximum_fusion.refs_0_), channel_id=1, source_target_pairs={{0,4},{1,33},{2,6},{3,35},{4,0},{5,37},{6,2},{7,39},{8,12},{9,41},... | collective-permute-start | bytes 786440 | tf_op jit(solution)/shard_map/ppermute | solution.py:51
  10.7 0.7 %collective-permute-start.6 = (bf16[512,256]{1,0:T(8,128)(2,1)S(1)}, bf16[512,256]{1,0:T(8,128)(2,1)S(1)}, u32[]{:S(2)}, u32[]{:S(2)}) collective-permute-start(bf16[512,256]{1,0:T(8,128)(2,1)S(1)} %pad_maximum_fusion.refs_0_), channel_id=1, source_target_pairs={{0,2},{1,17},{2,4},{3,19},{4,6},{5,21},{6,0},{7,23},{8,10},{9,25},... | collective-permute-start | bytes 786440 | tf_op jit(solution)/shard_map/ppermute | solution.py:51
  11.4 1.9 %collective-permute-start.7 = (bf16[512,256]{1,0:T(8,128)(2,1)S(1)}, bf16[512,256]{1,0:T(8,128)(2,1)S(1)}, u32[]{:S(2)}, u32[]{:S(2)}) collective-permute-start(bf16[512,256]{1,0:T(8,128)(2,1)S(1)} %pad_maximum_fusion.refs_0_), channel_id=1, source_target_pairs={{0,6},{1,49},{2,0},{3,51},{4,2},{5,53},{6,4},{7,55},{8,14},{9,57},... | collective-permute-start | bytes 786440 | tf_op jit(solution)/shard_map/ppermute | solution.py:51
  13.4 0.0 copy-done.1
  13.4 1.0 %collective-permute-start.10 = (bf16[128,1024]{1,0:T(8,128)(2,1)S(1)}, bf16[128,1024]{1,0:T(8,128)(2,1)S(1)}, u32[]{:S(2)}, u32[]{:S(2)}) collective-permute-start(bf16[128,1024]{1,0:T(8,128)(2,1)S(1)} %copy-done.1), channel_id=1, source_target_pairs={{0,8},{1,9},{2,10},{3,11},{4,12},{5,13},{6,14},{7,15},{8,0},{9,1},... | collective-permute-start | bytes 786440 | tf_op jit(solution)/shard_map/ppermute | solution.py:51
  14.4 2.0 %collective-permute-start.3 = (bf16[512,256]{1,0:T(8,128)(2,1)S(1)}, bf16[512,256]{1,0:T(8,128)(2,1)S(1)}, u32[]{:S(2)}, u32[]{:S(2)}) collective-permute-start(bf16[512,256]{1,0:T(8,128)(2,1)S(1)} %pad_maximum_fusion.refs_0_), channel_id=1, source_target_pairs={{0,1},{1,0},{2,3},{3,2},{4,5},{5,4},{6,7},{7,6},{8,9},{9,8},{10,11... | collective-permute-start | bytes 786440 | tf_op jit(solution)/shard_map/ppermute | solution.py:51
  16.4 0.0 collective-permute-done.4.refs_2_.refs_0_
  16.4 3.1 %collective-permute-start.5 = (bf16[512,256]{1,0:T(8,128)(2,1)S(1)}, bf16[512,256]{1,0:T(8,128)(2,1)S(1)}, u32[]{:S(2)}, u32[]{:S(2)}) collective-permute-start(bf16[512,256]{1,0:T(8,128)(2,1)S(1)} %collective-permute-done.4.refs_2_.refs_0_), channel_id=1, source_target_pairs={{0,1},{1,0},{2,3},{3,2},{4,5},{5,4},{6,7},{7,6},{8,9},{9,8},{10,11... | collective-permute-start | bytes 786440 | tf_op jit(solution)/shard_map/ppermute | solution.py:51
  19.4 0.0 collective-permute-done.6.refs_4_.refs_1_
  19.4 0.6 %collective-permute-start.8 = (bf16[512,256]{1,0:T(8,128)(2,1)S(1)}, bf16[512,256]{1,0:T(8,128)(2,1)S(1)}, u32[]{:S(2)}, u32[]{:S(2)}) collective-permute-start(bf16[512,256]{1,0:T(8,128)(2,1)S(1)} %collective-permute-done.6.refs_4_.refs_1_), channel_id=1, source_target_pairs={{0,1},{1,0},{2,3},{3,2},{4,5},{5,4},{6,7},{7,6},{8,9},{9,8},{10,11... | collective-permute-start | bytes 786440 | tf_op jit(solution)/shard_map/ppermute | solution.py:51
  20.0 0.0 collective-permute-done.7.refs_5_.refs_2_
  20.1 2.6 %collective-permute-start.9 = (bf16[512,256]{1,0:T(8,128)(2,1)S(1)}, bf16[512,256]{1,0:T(8,128)(2,1)S(1)}, u32[]{:S(2)}, u32[]{:S(2)}) collective-permute-start(bf16[512,256]{1,0:T(8,128)(2,1)S(1)} %collective-permute-done.7.refs_5_.refs_2_), channel_id=1, source_target_pairs={{0,1},{1,0},{2,3},{3,2},{4,5},{5,4},{6,7},{7,6},{8,9},{9,8},{10,11... | collective-permute-start | bytes 786440 | tf_op jit(solution)/shard_map/ppermute | solution.py:51
  22.6 0.0 copy-done
  22.6 1.7 %lists.1.table_ref = s32[8,128]{1,0:T(8,128)S(1)} custom-call(s32[64]{0:T(128)S(1)} %copy-done), custom_call_target="tpu_custom_call" | custom-call | flops 1024 | bytes 1024 | tf_op jit(solution)/shard_map/lists/pallas_call | solution.py:116
  24.3 0.0 collective-permute-done.10.queries_ref
  24.4 0.0 collective-permute-done.3.refs_1_
  24.4 1.8 %shard_map.47 = (f32[1024,128]{1,0:T(8,128)S(1)}, f32[1024,256]{1,0:T(8,128)S(1)}, bf16[1024,256]{1,0:T(8,128)(2,1)S(1)}) custom-call(s32[8,128]{1,0:T(8,128)S(1)} %lists.1.table_ref, bf16[128,1024]{1,0:T(8,128)(2,1)S(1)} %collective-permute-done.10.queries_ref, bf16[512,256]{1,0:T(8,128)(2,1)S(1)} %pad_maximum_fusion.refs_0_, ...), custom_call_target="tpu_custom_call" | custom-call | flops 536870912 | bytes 524288 | tf_op jit(solution)/shard_map/pallas_call | solution.py:365
  26.2 1.9 %shard_map.48 = (f32[1024,128]{1,0:T(8,128)S(1)}, f32[1024,256]{1,0:T(8,128)S(1)}) custom-call(s32[8,128]{1,0:T(8,128)S(1)} %lists.1.table_ref, bf16[1024,256]{1,0:T(8,128)(2,1)S(1)} %get-tuple-element.16.queries_ref, bf16[512,256]{1,0:T(8,128)(2,1)S(1)} %collective-permute-done.4.refs_2_.refs_0_, f32[1024,128]{1,0:T(8,128)S(1)} %get-tuple-element.17.refs_1_, ...), custom_call_target="tpu_custom_call" | custom-call | flops 268435456 | bytes 262144 | tf_op jit(solution)/shard_map/pallas_call | solution.py:365
  28.1 0.0 collective-permute-done.5.refs_3_.refs_0_
  28.1 2.8 %shard_map.49 = (f32[1024,128]{1,0:T(8,128)S(1)}, f32[1024,256]{1,0:T(8,128)S(1)}) custom-call(s32[8,128]{1,0:T(8,128)S(1)} %lists.1.table_ref, bf16[1024,256]{1,0:T(8,128)(2,1)S(1)} %get-tuple-element.16.queries_ref, bf16[512,256]{1,0:T(8,128)(2,1)S(1)} %collective-permute-done.5.refs_3_.refs_0_, ...), custom_call_target="tpu_custom_call" | custom-call | flops 805306368 | bytes 786432 | tf_op jit(solution)/shard_map/pallas_call | solution.py:365
  30.9 0.0 collective-permute-done.8.refs_6_.refs_0_
  30.9 0.0 collective-permute-done.9.refs_7_.refs_1_
  30.9 2.8 %shard_map.50 = bf16[1056,128]{1,0:T(8,128)(2,1)S(1)} custom-call(s32[8,128]{1,0:T(8,128)S(1)} %lists.1.table_ref, bf16[1024,256]{1,0:T(8,128)(2,1)S(1)} %get-tuple-element.16.queries_ref, bf16[512,256]{1,0:T(8,128)(2,1)S(1)} %collective-permute-done.8.refs_6_.refs_0_, bf16[512,256]{1,0:T(8,128)(2,1)S(1)} %collective-permute-done.9.refs_7_.refs_1_, ...), custom_call_target="tpu_custom_call" | custom-call | flops 536870912 | bytes 524288 | tf_op jit(solution)/shard_map/pallas_call | solution.py:365
  33.6 0.1 collective-permute-start.11
  33.7 3.3 %shard_map.46 = (f32[1024,128]{1,0:T(8,128)S(1)}, f32[128,128]{1,0:T(8,128)S(1)}) custom-call(s32[8,128]{1,0:T(8,128)S(1)} %lists.1.table_ref, bf16[128,1024]{1,0:T(8,128)(2,1)S(1)} %copy-done.1, bf16[512,256]{1,0:T(8,128)(2,1)S(1)} %pad_maximum_fusion.refs_0_, bf16[512,256]{1,0:T(8,128)(2,1)S(1)} %collective-permute-done.3.refs_1_, ...), custom_call_target="tpu_custom_call" | custom-call | flops 2147483648 | bytes 2097152 | tf_op jit(solution)/shard_map/pallas_call | solution.py:365
  37.0 4.9 %collective-permute-done.11.beside_ref = bf16[1056,128]{1,0:T(8,128)(2,1)S(1)} collective-permute-done((bf16[1056,128]{1,0:T(8,128)(2,1)S(1)}, bf16[1056,128]{1,0:T(8,128)(2,1)S(1)}, u32[]{:S(2)}, u32[]{:S(2)}) %collective-permute-start.11) | collective-permute-done | bytes 270368 | tf_op jit(solution)/shard_map/ppermute | solution.py:51
  41.9 1.2 %merge.1 = f32[128,1024]{1,0:T(8,128)} custom-call(f32[1024,128]{1,0:T(8,128)S(1)} %get-tuple-element.14.sums_ref, f32[128,128]{1,0:T(8,128)S(1)} %get-tuple-element.15.stats_ref, bf16[1056,128]{1,0:T(8,128)(2,1)S(1)} %collective-permute-done.11.beside_ref), custom_call_target="tpu_custom_call" | custom-call | flops 1048576 | bytes 2097152 | tf_op jit(solution)/shard_map/merge/pallas_call | solution.py:399
  (2 shorter events, 0.0 us)
Async XLA Ops:
  0.8 12.6 %copy-start.1 = (bf16[128,1024]{1,0:T(8,128)(2,1)S(1)}, bf16[128,1024]{1,0:T(8,128)(2,1)}, u32[]{:S(2)}) copy-start(bf16[128,1024]{1,0:T(8,128)(2,1)} %queries_ref.1) | copy-start | bytes 786436
  0.8 21.8 %copy-start = (s32[64]{0:T(128)S(1)}, s32[64]{0:T(128)}, u32[]{:S(2)}) copy-start(s32[64]{0:T(128)} %order_ref.1) | copy-start | bytes 772
  0.8 3.2 %collective-permute-start = (bf16[128,256]{1,0:T(8,128)(2,1)S(1)}, bf16[128,256]{1,0:T(8,128)(2,1)S(1)}, u32[]{:S(2)}, u32[]{:S(2)}) collective-permute-start(bf16[128,256]{1,0:T(8,128)(2,1)S(1)} %pad_select_fusion), channel_id=1, source_target_pairs={{0,16},{1,3},{2,18},{3,5},{4,20},{5,7},{6,22},{7,1},{8,24},{9,11},... | collective-permute-start | bytes 196616 | tf_op jit(solution)/shard_map/ppermute | solution.py:51
  1.1 4.3 %collective-permute-start.1 = (bf16[128,256]{1,0:T(8,128)(2,1)S(1)}, bf16[128,256]{1,0:T(8,128)(2,1)S(1)}, u32[]{:S(2)}, u32[]{:S(2)}) collective-permute-start(bf16[128,256]{1,0:T(8,128)(2,1)S(1)} %pad_select_fusion), channel_id=1, source_target_pairs={{0,48},{1,7},{2,50},{3,1},{4,52},{5,3},{6,54},{7,5},{8,56},{9,15},... | collective-permute-start | bytes 196616 | tf_op jit(solution)/shard_map/ppermute | solution.py:51
  2.4 4.6 %collective-permute-start.2 = (bf16[128,256]{1,0:T(8,128)(2,1)S(1)}, bf16[128,256]{1,0:T(8,128)(2,1)S(1)}, u32[]{:S(2)}, u32[]{:S(2)}) collective-permute-start(bf16[128,256]{1,0:T(8,128)(2,1)S(1)} %pad_select_fusion), channel_id=1, source_target_pairs={{0,32},{1,5},{2,34},{3,7},{4,36},{5,1},{6,38},{7,3},{8,40},{9,13},... | collective-permute-start | bytes 196616 | tf_op jit(solution)/shard_map/ppermute | solution.py:51
  7.0 9.4 %collective-permute-start.4 = (bf16[512,256]{1,0:T(8,128)(2,1)S(1)}, bf16[512,256]{1,0:T(8,128)(2,1)S(1)}, u32[]{:S(2)}, u32[]{:S(2)}) collective-permute-start(bf16[512,256]{1,0:T(8,128)(2,1)S(1)} %pad_maximum_fusion.refs_0_), channel_id=1, source_target_pairs={{0,4},{1,33},{2,6},{3,35},{4,0},{5,37},{6,2},{7,39},{8,12},{9,41},... | collective-permute-start | bytes 786440 | tf_op jit(solution)/shard_map/ppermute | solution.py:51
  10.7 8.8 %collective-permute-start.6 = (bf16[512,256]{1,0:T(8,128)(2,1)S(1)}, bf16[512,256]{1,0:T(8,128)(2,1)S(1)}, u32[]{:S(2)}, u32[]{:S(2)}) collective-permute-start(bf16[512,256]{1,0:T(8,128)(2,1)S(1)} %pad_maximum_fusion.refs_0_), channel_id=1, source_target_pairs={{0,2},{1,17},{2,4},{3,19},{4,6},{5,21},{6,0},{7,23},{8,10},{9,25},... | collective-permute-start | bytes 786440 | tf_op jit(solution)/shard_map/ppermute | solution.py:51
  11.4 8.6 %collective-permute-start.7 = (bf16[512,256]{1,0:T(8,128)(2,1)S(1)}, bf16[512,256]{1,0:T(8,128)(2,1)S(1)}, u32[]{:S(2)}, u32[]{:S(2)}) collective-permute-start(bf16[512,256]{1,0:T(8,128)(2,1)S(1)} %pad_maximum_fusion.refs_0_), channel_id=1, source_target_pairs={{0,6},{1,49},{2,0},{3,51},{4,2},{5,53},{6,4},{7,55},{8,14},{9,57},... | collective-permute-start | bytes 786440 | tf_op jit(solution)/shard_map/ppermute | solution.py:51
  13.4 11.0 %collective-permute-start.10 = (bf16[128,1024]{1,0:T(8,128)(2,1)S(1)}, bf16[128,1024]{1,0:T(8,128)(2,1)S(1)}, u32[]{:S(2)}, u32[]{:S(2)}) collective-permute-start(bf16[128,1024]{1,0:T(8,128)(2,1)S(1)} %copy-done.1), channel_id=1, source_target_pairs={{0,8},{1,9},{2,10},{3,11},{4,12},{5,13},{6,14},{7,15},{8,0},{9,1},... | collective-permute-start | bytes 786440 | tf_op jit(solution)/shard_map/ppermute | solution.py:51
  14.4 10.0 %collective-permute-start.3 = (bf16[512,256]{1,0:T(8,128)(2,1)S(1)}, bf16[512,256]{1,0:T(8,128)(2,1)S(1)}, u32[]{:S(2)}, u32[]{:S(2)}) collective-permute-start(bf16[512,256]{1,0:T(8,128)(2,1)S(1)} %pad_maximum_fusion.refs_0_), channel_id=1, source_target_pairs={{0,1},{1,0},{2,3},{3,2},{4,5},{5,4},{6,7},{7,6},{8,9},{9,8},{10,11... | collective-permute-start | bytes 786440 | tf_op jit(solution)/shard_map/ppermute | solution.py:51
  16.4 11.7 %collective-permute-start.5 = (bf16[512,256]{1,0:T(8,128)(2,1)S(1)}, bf16[512,256]{1,0:T(8,128)(2,1)S(1)}, u32[]{:S(2)}, u32[]{:S(2)}) collective-permute-start(bf16[512,256]{1,0:T(8,128)(2,1)S(1)} %collective-permute-done.4.refs_2_.refs_0_), channel_id=1, source_target_pairs={{0,1},{1,0},{2,3},{3,2},{4,5},{5,4},{6,7},{7,6},{8,9},{9,8},{10,11... | collective-permute-start | bytes 786440 | tf_op jit(solution)/shard_map/ppermute | solution.py:51
  19.4 11.4 %collective-permute-start.8 = (bf16[512,256]{1,0:T(8,128)(2,1)S(1)}, bf16[512,256]{1,0:T(8,128)(2,1)S(1)}, u32[]{:S(2)}, u32[]{:S(2)}) collective-permute-start(bf16[512,256]{1,0:T(8,128)(2,1)S(1)} %collective-permute-done.6.refs_4_.refs_1_), channel_id=1, source_target_pairs={{0,1},{1,0},{2,3},{3,2},{4,5},{5,4},{6,7},{7,6},{8,9},{9,8},{10,11... | collective-permute-start | bytes 786440 | tf_op jit(solution)/shard_map/ppermute | solution.py:51
  20.1 10.8 %collective-permute-start.9 = (bf16[512,256]{1,0:T(8,128)(2,1)S(1)}, bf16[512,256]{1,0:T(8,128)(2,1)S(1)}, u32[]{:S(2)}, u32[]{:S(2)}) collective-permute-start(bf16[512,256]{1,0:T(8,128)(2,1)S(1)} %collective-permute-done.7.refs_5_.refs_2_), channel_id=1, source_target_pairs={{0,1},{1,0},{2,3},{3,2},{4,5},{5,4},{6,7},{7,6},{8,9},{9,8},{10,11... | collective-permute-start | bytes 786440 | tf_op jit(solution)/shard_map/ppermute | solution.py:51
  33.6 8.3 %collective-permute-start.11 = (bf16[1056,128]{1,0:T(8,128)(2,1)S(1)}, bf16[1056,128]{1,0:T(8,128)(2,1)S(1)}, u32[]{:S(2)}, u32[]{:S(2)}) collective-permute-start(bf16[1056,128]{1,0:T(8,128)(2,1)S(1)} %shard_map.50), channel_id=1, source_target_pairs={{0,8},{1,9},{2,10},{3,11},{4,12},{5,13},{6,14},{7,15},{8,0},{9,1},... | collective-permute-start | bytes 811016 | tf_op jit(solution)/shard_map/ppermute | solution.py:51

commit v2 on v1

--- a/solution.py
+++ b/solution.py
@@ -416,7 +416,7 @@
 def attention(queries, keys, values, span_order):
     beside = send(queries, ACROSS_Y)
     kv = together(keys, values)
-    by_a, by_b, also_b = {}, {}, {}
+    by_a, by_b = {}, {}
     for d in (2, -1, 1):
         by_a[d] = send(kv, along_a(-d))
     table = lists(span_order)
@@ -424,13 +424,15 @@
     also_plane = send(plane, ACROSS_CORE)
     for d in (2, -1, 1):
         by_b[d] = send(plane, along_b(-d))
-        also_b[d] = send(by_b[d], ACROSS_CORE)
+    also_far = send(by_b[2], ACROSS_CORE)
+    sides = jnp.concatenate([by_b[-1], by_b[1]], axis=0)
+    also_sides = send(sides, ACROSS_CORE)
     *state, split = attend(0, STATE, table, beside, [plane, also_plane])
     state = attend(1, STATE, table, split, [by_b[2]], state)
-    state = attend(2, STATE, table, split, [also_b[2], by_b[-1], by_b[1]], state)
-    (packet,) = attend(3, PACKET, table, split, [also_b[-1], also_b[1]], state)
+    state = attend(2, STATE, table, split, [also_far, sides], state)
+    (packet,) = attend(3, PACKET, table, split, [also_sides], state)
     back = send(packet, ACROSS_Y)
-    arrays = [plane, also_plane, by_b[2], also_b[2], by_b[-1], by_b[1], also_b[-1], also_b[1]]
+    arrays = [plane, also_plane, by_b[2], also_far, sides, also_sides]
     sums, stats = attend(4, RESULT, table, queries, arrays)
     return merged(sums, stats, back)
 

time: 43.4 us -> 49.2 us (1.13)
  the two profiles are of different devices: /device:TPU:23 before, /device:TPU:22 now
where the time goes in v2:
time: 49.2 us; the launch traced here: 49 us
  waiting for transfers between devices  22.3 us (45%)
  Pallas kernels  14.1 us (29%)
  starting transfers between devices  11.5 us (23%)
  other arithmetic  0.81 us (2%)
    ppermute x11, waiting for transfers between devices, send(): return lax.ppermute(x, AXES, perm)  22.3 us
    ppermute x11, starting transfers between devices, send(): return lax.ppermute(x, AXES, perm)  11.5 us
    pallas_call x5, Pallas kernels, attend(): pl.pallas_call(functools.partial(attend_kernel, u, len(arrays), len(state...  11.2 us
    pallas_call x1, Pallas kernels, lists(): pl.pallas_call(lists_kernel, out_shape=jax.ShapeDtypeStruct((TABLE, STEPS...  1.69 us
    pallas_call x1, Pallas kernels, merged(): pl.pallas_call(merge_kernel, out_shape=jax.ShapeDtypeStruct((SPAN, HEADS...  1.16 us
  transfers between devices with their start and end apart: 11, of which 6 were waited for; matrix products, arithmetic and copies ran while one was open for 0% of the time, Pallas kernels for 22%

profile of v2, /device:TPU:22, one launch (start us, length us, event | category | flops | bytes accessed | tf_op | source)
XLA Modules:
  0.0 49.0 jit_solution(10030302407516122682)
XLA Ops:
  0.0 0.8 %pad_select_fusion = bf16[128,256]{1,0:T(8,128)(2,1)S(1)} fusion(bf16[128,128]{1,0:T(8,128)(2,1)} %param.6, bf16[128,128]{1,0:T(8,128)(2,1)} %param.5, pred[256]{0:T(512)(128)(4,1)S(1)} %iota_compare_fusion), kind=kLoop, calls=%fused_computation.1 | loop fusion | flops 32768 | bytes 131328 | tf_op jit(solution)/shard_map/jit(_where)/select_n | solution.py:413
  0.8 2.0 %collective-permute-start = (bf16[128,256]{1,0:T(8,128)(2,1)S(1)}, bf16[128,256]{1,0:T(8,128)(2,1)S(1)}, u32[]{:S(2)}, u32[]{:S(2)}) collective-permute-start(bf16[128,256]{1,0:T(8,128)(2,1)S(1)} %pad_select_fusion), channel_id=1, source_target_pairs={{0,16},{1,3},{2,18},{3,5},{4,20},{5,7},{6,22},{7,1},{8,24},{9,11},... | collective-permute-start | bytes 196616 | tf_op jit(solution)/shard_map/ppermute | solution.py:51
  2.8 2.2 %collective-permute-start.1 = (bf16[128,256]{1,0:T(8,128)(2,1)S(1)}, bf16[128,256]{1,0:T(8,128)(2,1)S(1)}, u32[]{:S(2)}, u32[]{:S(2)}) collective-permute-start(bf16[128,256]{1,0:T(8,128)(2,1)S(1)} %pad_select_fusion), channel_id=1, source_target_pairs={{0,48},{1,7},{2,50},{3,1},{4,52},{5,3},{6,54},{7,5},{8,56},{9,15},... | collective-permute-start | bytes 196616 | tf_op jit(solution)/shard_map/ppermute | solution.py:51
  5.0 1.8 %collective-permute-start.2 = (bf16[128,256]{1,0:T(8,128)(2,1)S(1)}, bf16[128,256]{1,0:T(8,128)(2,1)S(1)}, u32[]{:S(2)}, u32[]{:S(2)}) collective-permute-start(bf16[128,256]{1,0:T(8,128)(2,1)S(1)} %pad_select_fusion), channel_id=1, source_target_pairs={{0,32},{1,5},{2,34},{3,7},{4,36},{5,1},{6,38},{7,3},{8,40},{9,13},... | collective-permute-start | bytes 196616 | tf_op jit(solution)/shard_map/ppermute | solution.py:51
  6.8 0.4 collective-permute-done
  7.2 0.0 collective-permute-done.1
  7.2 3.6 %collective-permute-done.2 = bf16[128,256]{1,0:T(8,128)(2,1)S(1)} collective-permute-done((bf16[128,256]{1,0:T(8,128)(2,1)S(1)}, bf16[128,256]{1,0:T(8,128)(2,1)S(1)}, u32[]{:S(2)}, u32[]{:S(2)}) %collective-permute-start.2) | collective-permute-done | bytes 65568 | tf_op jit(solution)/shard_map/ppermute | solution.py:51
  10.8 0.5 %collective-permute-start.6 = (bf16[512,256]{1,0:T(8,128)(2,1)S(1)}, bf16[512,256]{1,0:T(8,128)(2,1)S(1)}, u32[]{:S(2)}, u32[]{:S(2)}) collective-permute-start(bf16[512,256]{1,0:T(8,128)(2,1)S(1)} %pad_maximum_fusion.refs_0_), channel_id=1, source_target_pairs={{0,2},{1,17},{2,4},{3,19},{4,6},{5,21},{6,0},{7,23},{8,10},{9,25},... | collective-permute-start | bytes 786440 | tf_op jit(solution)/shard_map/ppermute | solution.py:51
  11.3 1.5 %collective-permute-start.7 = (bf16[512,256]{1,0:T(8,128)(2,1)S(1)}, bf16[512,256]{1,0:T(8,128)(2,1)S(1)}, u32[]{:S(2)}, u32[]{:S(2)}) collective-permute-start(bf16[512,256]{1,0:T(8,128)(2,1)S(1)} %pad_maximum_fusion.refs_0_), channel_id=1, source_target_pairs={{0,6},{1,49},{2,0},{3,51},{4,2},{5,53},{6,4},{7,55},{8,14},{9,57},... | collective-permute-start | bytes 786440 | tf_op jit(solution)/shard_map/ppermute | solution.py:51
  12.9 1.4 %collective-permute-start.4 = (bf16[512,256]{1,0:T(8,128)(2,1)S(1)}, bf16[512,256]{1,0:T(8,128)(2,1)S(1)}, u32[]{:S(2)}, u32[]{:S(2)}) collective-permute-start(bf16[512,256]{1,0:T(8,128)(2,1)S(1)} %pad_maximum_fusion.refs_0_), channel_id=1, source_target_pairs={{0,4},{1,33},{2,6},{3,35},{4,0},{5,37},{6,2},{7,39},{8,12},{9,41},... | collective-permute-start | bytes 786440 | tf_op jit(solution)/shard_map/ppermute | solution.py:51
  14.3 2.9 %collective-permute-done.6 = bf16[512,256]{1,0:T(8,128)(2,1)S(1)} collective-permute-done((bf16[512,256]{1,0:T(8,128)(2,1)S(1)}, bf16[512,256]{1,0:T(8,128)(2,1)S(1)}, u32[]{:S(2)}, u32[]{:S(2)}) %collective-permute-start.6) | collective-permute-done | bytes 262176 | tf_op jit(solution)/shard_map/ppermute | solution.py:51
  17.2 0.0 copy-start.1
  17.3 0.0 copy-start
  17.3 4.5 %collective-permute-done.7 = bf16[512,256]{1,0:T(8,128)(2,1)S(1)} collective-permute-done((bf16[512,256]{1,0:T(8,128)(2,1)S(1)}, bf16[512,256]{1,0:T(8,128)(2,1)S(1)}, u32[]{:S(2)}, u32[]{:S(2)}) %collective-permute-start.7) | collective-permute-done | bytes 262176 | tf_op jit(solution)/shard_map/ppermute | solution.py:51
  21.7 0.1 collective-permute-start.8
  21.8 0.0 copy-done.1
  21.8 1.4 %collective-permute-start.9 = (bf16[128,1024]{1,0:T(8,128)(2,1)S(1)}, bf16[128,1024]{1,0:T(8,128)(2,1)S(1)}, u32[]{:S(2)}, u32[]{:S(2)}) collective-permute-start(bf16[128,1024]{1,0:T(8,128)(2,1)S(1)} %copy-done.1), channel_id=1, source_target_pairs={{0,8},{1,9},{2,10},{3,11},{4,12},{5,13},{6,14},{7,15},{8,0},{9,1},... | collective-permute-start | bytes 786440 | tf_op jit(solution)/shard_map/ppermute | solution.py:51
  23.2 0.1 collective-permute-start.3
  23.3 0.0 collective-permute-done.4.refs_2_.refs_0_
  23.3 0.4 collective-permute-start.5
  23.7 0.0 copy-done
  23.7 1.7 %lists.1.table_ref = s32[8,128]{1,0:T(8,128)S(1)} custom-call(s32[64]{0:T(128)S(1)} %copy-done), custom_call_target="tpu_custom_call" | custom-call | flops 1024 | bytes 1024 | tf_op jit(solution)/shard_map/lists/pallas_call | solution.py:116
  25.4 5.1 %collective-permute-done.9.queries_ref = bf16[128,1024]{1,0:T(8,128)(2,1)S(1)} collective-permute-done((bf16[128,1024]{1,0:T(8,128)(2,1)S(1)}, bf16[128,1024]{1,0:T(8,128)(2,1)S(1)}, u32[]{:S(2)}, u32[]{:S(2)}) %collective-permute-start.9) | collective-permute-done | bytes 262176 | tf_op jit(solution)/shard_map/ppermute | solution.py:51
  30.5 0.0 collective-permute-done.3.refs_1_
  30.5 1.9 %shard_map.47 = (f32[1024,128]{1,0:T(8,128)S(1)}, f32[1024,256]{1,0:T(8,128)S(1)}, bf16[1024,256]{1,0:T(8,128)(2,1)S(1)}) custom-call(s32[8,128]{1,0:T(8,128)S(1)} %lists.1.table_ref, bf16[128,1024]{1,0:T(8,128)(2,1)S(1)} %collective-permute-done.9.queries_ref, bf16[512,256]{1,0:T(8,128)(2,1)S(1)} %pad_maximum_fusion.refs_0_, ...), custom_call_target="tpu_custom_call" | custom-call | flops 536870912 | bytes 524288 | tf_op jit(solution)/shard_map/pallas_call | solution.py:365
  32.4 1.9 %shard_map.48 = (f32[1024,128]{1,0:T(8,128)S(1)}, f32[1024,256]{1,0:T(8,128)S(1)}) custom-call(s32[8,128]{1,0:T(8,128)S(1)} %lists.1.table_ref, bf16[1024,256]{1,0:T(8,128)(2,1)S(1)} %get-tuple-element.16.queries_ref, bf16[512,256]{1,0:T(8,128)(2,1)S(1)} %collective-permute-done.4.refs_2_.refs_0_, f32[1024,128]{1,0:T(8,128)S(1)} %get-tuple-element.17.refs_1_, ...), custom_call_target="tpu_custom_call" | custom-call | flops 268435456 | bytes 262144 | tf_op jit(solution)/shard_map/pallas_call | solution.py:365
  34.3 0.0 collective-permute-done.5.refs_3_.refs_0_
  34.3 2.5 %shard_map.49 = (f32[1024,128]{1,0:T(8,128)S(1)}, f32[1024,256]{1,0:T(8,128)S(1)}) custom-call(s32[8,128]{1,0:T(8,128)S(1)} %lists.1.table_ref, bf16[1024,256]{1,0:T(8,128)(2,1)S(1)} %get-tuple-element.16.queries_ref, bf16[512,256]{1,0:T(8,128)(2,1)S(1)} %collective-permute-done.5.refs_3_.refs_0_, ...), custom_call_target="tpu_custom_call" | custom-call | flops 805306368 | bytes 786432 | tf_op jit(solution)/shard_map/pallas_call | solution.py:365
  36.8 0.0 collective-permute-done.8.refs_5_.refs_0_
  36.8 2.2 %shard_map.50 = bf16[1056,128]{1,0:T(8,128)(2,1)S(1)} custom-call(s32[8,128]{1,0:T(8,128)S(1)} %lists.1.table_ref, bf16[1024,256]{1,0:T(8,128)(2,1)S(1)} %get-tuple-element.16.queries_ref, bf16[1024,256]{1,0:T(8,128)(2,1)S(1)} %collective-permute-done.8.refs_5_.refs_0_, f32[1024,128]{1,0:T(8,128)S(1)} %get-tuple-element.21.refs_1_, ...), custom_call_target="tpu_custom_call" | custom-call | flops 536870912 | bytes 524288 | tf_op jit(solution)/shard_map/pallas_call | solution.py:365
  39.0 0.1 collective-permute-start.10
  39.1 2.8 %shard_map.46 = (f32[1024,128]{1,0:T(8,128)S(1)}, f32[128,128]{1,0:T(8,128)S(1)}) custom-call(s32[8,128]{1,0:T(8,128)S(1)} %lists.1.table_ref, bf16[128,1024]{1,0:T(8,128)(2,1)S(1)} %copy-done.1, bf16[512,256]{1,0:T(8,128)(2,1)S(1)} %pad_maximum_fusion.refs_0_, bf16[512,256]{1,0:T(8,128)(2,1)S(1)} %collective-permute-done.3.refs_1_, ...), custom_call_target="tpu_custom_call" | custom-call | flops 2147483648 | bytes 2097152 | tf_op jit(solution)/shard_map/pallas_call | solution.py:365
  41.9 5.8 %collective-permute-done.10.beside_ref = bf16[1056,128]{1,0:T(8,128)(2,1)S(1)} collective-permute-done((bf16[1056,128]{1,0:T(8,128)(2,1)S(1)}, bf16[1056,128]{1,0:T(8,128)(2,1)S(1)}, u32[]{:S(2)}, u32[]{:S(2)}) %collective-permute-start.10) | collective-permute-done | bytes 270368 | tf_op jit(solution)/shard_map/ppermute | solution.py:51
  47.7 1.2 %merge.1 = f32[128,1024]{1,0:T(8,128)} custom-call(f32[1024,128]{1,0:T(8,128)S(1)} %get-tuple-element.14.sums_ref, f32[128,128]{1,0:T(8,128)S(1)} %get-tuple-element.15.stats_ref, bf16[1056,128]{1,0:T(8,128)(2,1)S(1)} %collective-permute-done.10.beside_ref), custom_call_target="tpu_custom_call" | custom-call | flops 1048576 | bytes 2097152 | tf_op jit(solution)/shard_map/merge/pallas_call | solution.py:399
  (4 shorter events, 0.1 us)
Async XLA Ops:
  0.8 6.4 %collective-permute-start = (bf16[128,256]{1,0:T(8,128)(2,1)S(1)}, bf16[128,256]{1,0:T(8,128)(2,1)S(1)}, u32[]{:S(2)}, u32[]{:S(2)}) collective-permute-start(bf16[128,256]{1,0:T(8,128)(2,1)S(1)} %pad_select_fusion), channel_id=1, source_target_pairs={{0,16},{1,3},{2,18},{3,5},{4,20},{5,7},{6,22},{7,1},{8,24},{9,11},... | collective-permute-start | bytes 196616 | tf_op jit(solution)/shard_map/ppermute | solution.py:51
  2.8 4.4 %collective-permute-start.1 = (bf16[128,256]{1,0:T(8,128)(2,1)S(1)}, bf16[128,256]{1,0:T(8,128)(2,1)S(1)}, u32[]{:S(2)}, u32[]{:S(2)}) collective-permute-start(bf16[128,256]{1,0:T(8,128)(2,1)S(1)} %pad_select_fusion), channel_id=1, source_target_pairs={{0,48},{1,7},{2,50},{3,1},{4,52},{5,3},{6,54},{7,5},{8,56},{9,15},... | collective-permute-start | bytes 196616 | tf_op jit(solution)/shard_map/ppermute | solution.py:51
  5.0 5.8 %collective-permute-start.2 = (bf16[128,256]{1,0:T(8,128)(2,1)S(1)}, bf16[128,256]{1,0:T(8,128)(2,1)S(1)}, u32[]{:S(2)}, u32[]{:S(2)}) collective-permute-start(bf16[128,256]{1,0:T(8,128)(2,1)S(1)} %pad_select_fusion), channel_id=1, source_target_pairs={{0,32},{1,5},{2,34},{3,7},{4,36},{5,1},{6,38},{7,3},{8,40},{9,13},... | collective-permute-start | bytes 196616 | tf_op jit(solution)/shard_map/ppermute | solution.py:51
  10.8 6.4 %collective-permute-start.6 = (bf16[512,256]{1,0:T(8,128)(2,1)S(1)}, bf16[512,256]{1,0:T(8,128)(2,1)S(1)}, u32[]{:S(2)}, u32[]{:S(2)}) collective-permute-start(bf16[512,256]{1,0:T(8,128)(2,1)S(1)} %pad_maximum_fusion.refs_0_), channel_id=1, source_target_pairs={{0,2},{1,17},{2,4},{3,19},{4,6},{5,21},{6,0},{7,23},{8,10},{9,25},... | collective-permute-start | bytes 786440 | tf_op jit(solution)/shard_map/ppermute | solution.py:51
  11.3 10.4 %collective-permute-start.7 = (bf16[512,256]{1,0:T(8,128)(2,1)S(1)}, bf16[512,256]{1,0:T(8,128)(2,1)S(1)}, u32[]{:S(2)}, u32[]{:S(2)}) collective-permute-start(bf16[512,256]{1,0:T(8,128)(2,1)S(1)} %pad_maximum_fusion.refs_0_), channel_id=1, source_target_pairs={{0,6},{1,49},{2,0},{3,51},{4,2},{5,53},{6,4},{7,55},{8,14},{9,57},... | collective-permute-start | bytes 786440 | tf_op jit(solution)/shard_map/ppermute | solution.py:51
  12.9 10.5 %collective-permute-start.4 = (bf16[512,256]{1,0:T(8,128)(2,1)S(1)}, bf16[512,256]{1,0:T(8,128)(2,1)S(1)}, u32[]{:S(2)}, u32[]{:S(2)}) collective-permute-start(bf16[512,256]{1,0:T(8,128)(2,1)S(1)} %pad_maximum_fusion.refs_0_), channel_id=1, source_target_pairs={{0,4},{1,33},{2,6},{3,35},{4,0},{5,37},{6,2},{7,39},{8,12},{9,41},... | collective-permute-start | bytes 786440 | tf_op jit(solution)/shard_map/ppermute | solution.py:51
  17.2 4.6 %copy-start.1 = (bf16[128,1024]{1,0:T(8,128)(2,1)S(1)}, bf16[128,1024]{1,0:T(8,128)(2,1)}, u32[]{:S(2)}) copy-start(bf16[128,1024]{1,0:T(8,128)(2,1)} %queries_ref.1) | copy-start | bytes 786436
  17.3 6.5 %copy-start = (s32[64]{0:T(128)S(1)}, s32[64]{0:T(128)}, u32[]{:S(2)}) copy-start(s32[64]{0:T(128)} %order_ref.1) | copy-start | bytes 772
  21.7 15.0 %collective-permute-start.8 = (bf16[1024,256]{1,0:T(8,128)(2,1)S(1)}, bf16[1024,256]{1,0:T(8,128)(2,1)S(1)}, u32[]{:S(2)}, u32[]{:S(2)}) collective-permute-start(bf16[1024,256]{1,0:T(8,128)(2,1)S(1)} %constant_dynamic-update-slice_fusion.refs_4_.refs_1_), channel_id=1, source_target_pairs={{0,1},{1,0},{2,3},{3,2},{4,5},{5,4},{6,7},{7,6},{8,9},{9,8},{10,11... | collective-permute-start | bytes 1572872 | tf_op jit(solution)/shard_map/ppermute | solution.py:51
  21.8 8.7 %collective-permute-start.9 = (bf16[128,1024]{1,0:T(8,128)(2,1)S(1)}, bf16[128,1024]{1,0:T(8,128)(2,1)S(1)}, u32[]{:S(2)}, u32[]{:S(2)}) collective-permute-start(bf16[128,1024]{1,0:T(8,128)(2,1)S(1)} %copy-done.1), channel_id=1, source_target_pairs={{0,8},{1,9},{2,10},{3,11},{4,12},{5,13},{6,14},{7,15},{8,0},{9,1},... | collective-permute-start | bytes 786440 | tf_op jit(solution)/shard_map/ppermute | solution.py:51
  23.2 7.3 %collective-permute-start.3 = (bf16[512,256]{1,0:T(8,128)(2,1)S(1)}, bf16[512,256]{1,0:T(8,128)(2,1)S(1)}, u32[]{:S(2)}, u32[]{:S(2)}) collective-permute-start(bf16[512,256]{1,0:T(8,128)(2,1)S(1)} %pad_maximum_fusion.refs_0_), channel_id=1, source_target_pairs={{0,1},{1,0},{2,3},{3,2},{4,5},{5,4},{6,7},{7,6},{8,9},{9,8},{10,11... | collective-permute-start | bytes 786440 | tf_op jit(solution)/shard_map/ppermute | solution.py:51
  23.3 10.9 %collective-permute-start.5 = (bf16[512,256]{1,0:T(8,128)(2,1)S(1)}, bf16[512,256]{1,0:T(8,128)(2,1)S(1)}, u32[]{:S(2)}, u32[]{:S(2)}) collective-permute-start(bf16[512,256]{1,0:T(8,128)(2,1)S(1)} %collective-permute-done.4.refs_2_.refs_0_), channel_id=1, source_target_pairs={{0,1},{1,0},{2,3},{3,2},{4,5},{5,4},{6,7},{7,6},{8,9},{9,8},{10,11... | collective-permute-start | bytes 786440 | tf_op jit(solution)/shard_map/ppermute | solution.py:51
  39.0 8.7 %collective-permute-start.10 = (bf16[1056,128]{1,0:T(8,128)(2,1)S(1)}, bf16[1056,128]{1,0:T(8,128)(2,1)S(1)}, u32[]{:S(2)}, u32[]{:S(2)}) collective-permute-start(bf16[1056,128]{1,0:T(8,128)(2,1)S(1)} %shard_map.50), channel_id=1, source_target_pairs={{0,8},{1,9},{2,10},{3,11},{4,12},{5,13},{6,14},{7,15},{8,0},{9,1},... | collective-permute-start | bytes 811016 | tf_op jit(solution)/shard_map/ppermute | solution.py:51

commit v3 on v1

--- a/solution.py
+++ b/solution.py
@@ -73,8 +73,8 @@
 
 OWN, BESIDE = range(2)
 LISTS = (
-    (BESIDE, ring(0, 0) + ring(1, 0)),
-    (BESIDE, ring(0, 2)),
+    (BESIDE, ring(0, 0)),
+    (BESIDE, ring(1, 0) + ring(0, 2)),
     (BESIDE, ring(1, 2) + ring(0, -1) + ring(0, 1)),
     (BESIDE, ring(1, -1) + ring(1, 1)),
     (OWN, ring(0, 0) + ring(1, 0) + ring(0, 2) + ring(1, 2) + ring(0, -1) + ring(0, 1) + ring(1, -1) + ring(1, 1)),
@@ -425,8 +425,8 @@
     for d in (2, -1, 1):
         by_b[d] = send(plane, along_b(-d))
         also_b[d] = send(by_b[d], ACROSS_CORE)
-    *state, split = attend(0, STATE, table, beside, [plane, also_plane])
-    state = attend(1, STATE, table, split, [by_b[2]], state)
+    *state, split = attend(0, STATE, table, beside, [plane])
+    state = attend(1, STATE, table, split, [also_plane, by_b[2]], state)
     state = attend(2, STATE, table, split, [also_b[2], by_b[-1], by_b[1]], state)
     (packet,) = attend(3, PACKET, table, split, [also_b[-1], also_b[1]], state)
     back = send(packet, ACROSS_Y)

time: 43.4 us -> 43.6 us (level)
  the two profiles are of different devices: /device:TPU:23 before, /device:TPU:1 now
where the time goes in v3:
time: 43.6 us; the launch traced here: 43.4 us
  starting transfers between devices  19.4 us (44%)
  Pallas kernels  14.8 us (34%)
  waiting for transfers between devices  8.1 us (19%)
  other arithmetic  0.81 us (2%)
    ppermute x12, starting transfers between devices, send(): return lax.ppermute(x, AXES, perm)  19.4 us
    pallas_call x5, Pallas kernels, attend(): pl.pallas_call(functools.partial(attend_kernel, u, len(arrays), len(state...  11.9 us
    ppermute x12, waiting for transfers between devices, send(): return lax.ppermute(x, AXES, perm)  8.1 us
    pallas_call x1, Pallas kernels, lists(): pl.pallas_call(lists_kernel, out_shape=jax.ShapeDtypeStruct((TABLE, STEPS...  1.7 us
    pallas_call x1, Pallas kernels, merged(): pl.pallas_call(merge_kernel, out_shape=jax.ShapeDtypeStruct((SPAN, HEADS...  1.16 us
  transfers between devices with their start and end apart: 12, of which 3 were waited for; matrix products, arithmetic and copies ran while one was open for 0% of the time, Pallas kernels for 26%

profile of v3, /device:TPU:1, one launch (start us, length us, event | category | flops | bytes accessed | tf_op | source)
XLA Modules:
  0.0 43.4 jit_solution(6669004142657324930)
XLA Ops:
  0.0 0.8 %pad_select_fusion = bf16[128,256]{1,0:T(8,128)(2,1)S(1)} fusion(bf16[128,128]{1,0:T(8,128)(2,1)} %param.6, bf16[128,128]{1,0:T(8,128)(2,1)} %param.5, pred[256]{0:T(512)(128)(4,1)S(1)} %iota_compare_fusion), kind=kLoop, calls=%fused_computation.1 | loop fusion | flops 32768 | bytes 131328 | tf_op jit(solution)/shard_map/jit(_where)/select_n | solution.py:413
  0.8 0.0 copy-start.1
  0.8 0.0 copy-start
  0.8 2.1 %collective-permute-start = (bf16[128,256]{1,0:T(8,128)(2,1)S(1)}, bf16[128,256]{1,0:T(8,128)(2,1)S(1)}, u32[]{:S(2)}, u32[]{:S(2)}) collective-permute-start(bf16[128,256]{1,0:T(8,128)(2,1)S(1)} %pad_select_fusion), channel_id=1, source_target_pairs={{0,16},{1,3},{2,18},{3,5},{4,20},{5,7},{6,22},{7,1},{8,24},{9,11},... | collective-permute-start | bytes 196616 | tf_op jit(solution)/shard_map/ppermute | solution.py:51
  2.9 1.4 %collective-permute-start.1 = (bf16[128,256]{1,0:T(8,128)(2,1)S(1)}, bf16[128,256]{1,0:T(8,128)(2,1)S(1)}, u32[]{:S(2)}, u32[]{:S(2)}) collective-permute-start(bf16[128,256]{1,0:T(8,128)(2,1)S(1)} %pad_select_fusion), channel_id=1, source_target_pairs={{0,48},{1,7},{2,50},{3,1},{4,52},{5,3},{6,54},{7,5},{8,56},{9,15},... | collective-permute-start | bytes 196616 | tf_op jit(solution)/shard_map/ppermute | solution.py:51
  4.3 1.6 %collective-permute-start.2 = (bf16[128,256]{1,0:T(8,128)(2,1)S(1)}, bf16[128,256]{1,0:T(8,128)(2,1)S(1)}, u32[]{:S(2)}, u32[]{:S(2)}) collective-permute-start(bf16[128,256]{1,0:T(8,128)(2,1)S(1)} %pad_select_fusion), channel_id=1, source_target_pairs={{0,32},{1,5},{2,34},{3,7},{4,36},{5,1},{6,38},{7,3},{8,40},{9,13},... | collective-permute-start | bytes 196616 | tf_op jit(solution)/shard_map/ppermute | solution.py:51
  5.9 0.0 collective-permute-done
  5.9 0.1 collective-permute-done.1
  6.0 2.9 %collective-permute-done.2 = bf16[128,256]{1,0:T(8,128)(2,1)S(1)} collective-permute-done((bf16[128,256]{1,0:T(8,128)(2,1)S(1)}, bf16[128,256]{1,0:T(8,128)(2,1)S(1)}, u32[]{:S(2)}, u32[]{:S(2)}) %collective-permute-start.2) | collective-permute-done | bytes 65568 | tf_op jit(solution)/shard_map/ppermute | solution.py:51
  8.9 3.8 %collective-permute-start.4 = (bf16[512,256]{1,0:T(8,128)(2,1)S(1)}, bf16[512,256]{1,0:T(8,128)(2,1)S(1)}, u32[]{:S(2)}, u32[]{:S(2)}) collective-permute-start(bf16[512,256]{1,0:T(8,128)(2,1)S(1)} %pad_maximum_fusion.refs_0_), channel_id=1, source_target_pairs={{0,4},{1,33},{2,6},{3,35},{4,0},{5,37},{6,2},{7,39},{8,12},{9,41},... | collective-permute-start | bytes 786440 | tf_op jit(solution)/shard_map/ppermute | solution.py:51
  12.7 1.0 %collective-permute-start.6 = (bf16[512,256]{1,0:T(8,128)(2,1)S(1)}, bf16[512,256]{1,0:T(8,128)(2,1)S(1)}, u32[]{:S(2)}, u32[]{:S(2)}) collective-permute-start(bf16[512,256]{1,0:T(8,128)(2,1)S(1)} %pad_maximum_fusion.refs_0_), channel_id=1, source_target_pairs={{0,2},{1,17},{2,4},{3,19},{4,6},{5,21},{6,0},{7,23},{8,10},{9,25},... | collective-permute-start | bytes 786440 | tf_op jit(solution)/shard_map/ppermute | solution.py:51
  13.7 1.6 %collective-permute-start.7 = (bf16[512,256]{1,0:T(8,128)(2,1)S(1)}, bf16[512,256]{1,0:T(8,128)(2,1)S(1)}, u32[]{:S(2)}, u32[]{:S(2)}) collective-permute-start(bf16[512,256]{1,0:T(8,128)(2,1)S(1)} %pad_maximum_fusion.refs_0_), channel_id=1, source_target_pairs={{0,6},{1,49},{2,0},{3,51},{4,2},{5,53},{6,4},{7,55},{8,14},{9,57},... | collective-permute-start | bytes 786440 | tf_op jit(solution)/shard_map/ppermute | solution.py:51
  15.4 0.0 copy-done.1
  15.4 1.3 %collective-permute-start.10 = (bf16[128,1024]{1,0:T(8,128)(2,1)S(1)}, bf16[128,1024]{1,0:T(8,128)(2,1)S(1)}, u32[]{:S(2)}, u32[]{:S(2)}) collective-permute-start(bf16[128,1024]{1,0:T(8,128)(2,1)S(1)} %copy-done.1), channel_id=1, source_target_pairs={{0,8},{1,9},{2,10},{3,11},{4,12},{5,13},{6,14},{7,15},{8,0},{9,1},... | collective-permute-start | bytes 786440 | tf_op jit(solution)/shard_map/ppermute | solution.py:51
  16.7 3.5 %collective-permute-start.3 = (bf16[512,256]{1,0:T(8,128)(2,1)S(1)}, bf16[512,256]{1,0:T(8,128)(2,1)S(1)}, u32[]{:S(2)}, u32[]{:S(2)}) collective-permute-start(bf16[512,256]{1,0:T(8,128)(2,1)S(1)} %pad_maximum_fusion.refs_0_), channel_id=1, source_target_pairs={{0,1},{1,0},{2,3},{3,2},{4,5},{5,4},{6,7},{7,6},{8,9},{9,8},{10,11... | collective-permute-start | bytes 786440 | tf_op jit(solution)/shard_map/ppermute | solution.py:51
  20.2 0.0 collective-permute-done.4.refs_2_.refs_1_
  20.2 0.0 collective-permute-start.5
  20.3 0.0 collective-permute-done.6.refs_4_.refs_1_
  20.3 2.8 %collective-permute-start.8 = (bf16[512,256]{1,0:T(8,128)(2,1)S(1)}, bf16[512,256]{1,0:T(8,128)(2,1)S(1)}, u32[]{:S(2)}, u32[]{:S(2)}) collective-permute-start(bf16[512,256]{1,0:T(8,128)(2,1)S(1)} %collective-permute-done.6.refs_4_.refs_1_), channel_id=1, source_target_pairs={{0,1},{1,0},{2,3},{3,2},{4,5},{5,4},{6,7},{7,6},{8,9},{9,8},{10,11... | collective-permute-start | bytes 786440 | tf_op jit(solution)/shard_map/ppermute | solution.py:51
  23.1 0.0 collective-permute-done.7.refs_5_.refs_2_
  23.1 0.1 collective-permute-start.9
  23.1 0.0 copy-done
  23.1 1.7 %lists.1.table_ref = s32[8,128]{1,0:T(8,128)S(1)} custom-call(s32[64]{0:T(128)S(1)} %copy-done), custom_call_target="tpu_custom_call" | custom-call | flops 1024 | bytes 1024 | tf_op jit(solution)/shard_map/lists/pallas_call | solution.py:116
  24.9 0.0 collective-permute-done.10.queries_ref
  24.9 1.9 %shard_map.47 = (f32[1024,128]{1,0:T(8,128)S(1)}, f32[1024,256]{1,0:T(8,128)S(1)}, bf16[1024,256]{1,0:T(8,128)(2,1)S(1)}) custom-call(s32[8,128]{1,0:T(8,128)S(1)} %lists.1.table_ref, bf16[128,1024]{1,0:T(8,128)(2,1)S(1)} %collective-permute-done.10.queries_ref, bf16[512,256]{1,0:T(8,128)(2,1)S(1)} %pad_maximum_fusion.refs_0_), custom_call_target="tpu_custom_call" | custom-call | flops 268435456 | bytes 262144 | tf_op jit(solution)/shard_map/pallas_call | solution.py:365
  26.7 0.0 collective-permute-done.3.refs_1_.refs_0_
  26.7 2.3 %shard_map.48 = (f32[1024,128]{1,0:T(8,128)S(1)}, f32[1024,256]{1,0:T(8,128)S(1)}) custom-call(s32[8,128]{1,0:T(8,128)S(1)} %lists.1.table_ref, bf16[1024,256]{1,0:T(8,128)(2,1)S(1)} %get-tuple-element.16.queries_ref, bf16[512,256]{1,0:T(8,128)(2,1)S(1)} %collective-permute-done.3.refs_1_.refs_0_, ...), custom_call_target="tpu_custom_call" | custom-call | flops 536870912 | bytes 524288 | tf_op jit(solution)/shard_map/pallas_call | solution.py:365
  29.0 0.0 collective-permute-done.5.refs_3_.refs_0_
  29.0 2.8 %shard_map.49 = (f32[1024,128]{1,0:T(8,128)S(1)}, f32[1024,256]{1,0:T(8,128)S(1)}) custom-call(s32[8,128]{1,0:T(8,128)S(1)} %lists.1.table_ref, bf16[1024,256]{1,0:T(8,128)(2,1)S(1)} %get-tuple-element.16.queries_ref, bf16[512,256]{1,0:T(8,128)(2,1)S(1)} %collective-permute-done.5.refs_3_.refs_0_, ...), custom_call_target="tpu_custom_call" | custom-call | flops 805306368 | bytes 786432 | tf_op jit(solution)/shard_map/pallas_call | solution.py:365
  31.8 0.0 collective-permute-done.8.refs_6_.refs_0_
  31.8 0.0 collective-permute-done.9.refs_7_.refs_1_
  31.8 2.4 %shard_map.50 = bf16[1056,128]{1,0:T(8,128)(2,1)S(1)} custom-call(s32[8,128]{1,0:T(8,128)S(1)} %lists.1.table_ref, bf16[1024,256]{1,0:T(8,128)(2,1)S(1)} %get-tuple-element.16.queries_ref, bf16[512,256]{1,0:T(8,128)(2,1)S(1)} %collective-permute-done.8.refs_6_.refs_0_, bf16[512,256]{1,0:T(8,128)(2,1)S(1)} %collective-permute-done.9.refs_7_.refs_1_, ...), custom_call_target="tpu_custom_call" | custom-call | flops 536870912 | bytes 524288 | tf_op jit(solution)/shard_map/pallas_call | solution.py:365
  34.3 0.1 collective-permute-start.11
  34.4 2.6 %shard_map.46 = (f32[1024,128]{1,0:T(8,128)S(1)}, f32[128,128]{1,0:T(8,128)S(1)}) custom-call(s32[8,128]{1,0:T(8,128)S(1)} %lists.1.table_ref, bf16[128,1024]{1,0:T(8,128)(2,1)S(1)} %copy-done.1, bf16[512,256]{1,0:T(8,128)(2,1)S(1)} %pad_maximum_fusion.refs_0_, bf16[512,256]{1,0:T(8,128)(2,1)S(1)} %collective-permute-done.3.refs_1_.refs_0_, ...), custom_call_target="tpu_custom_call" | custom-call | flops 2147483648 | bytes 2097152 | tf_op jit(solution)/shard_map/pallas_call | solution.py:365
  36.9 5.1 %collective-permute-done.11.beside_ref = bf16[1056,128]{1,0:T(8,128)(2,1)S(1)} collective-permute-done((bf16[1056,128]{1,0:T(8,128)(2,1)S(1)}, bf16[1056,128]{1,0:T(8,128)(2,1)S(1)}, u32[]{:S(2)}, u32[]{:S(2)}) %collective-permute-start.11) | collective-permute-done | bytes 270368 | tf_op jit(solution)/shard_map/ppermute | solution.py:51
  42.1 1.2 %merge.1 = f32[128,1024]{1,0:T(8,128)} custom-call(f32[1024,128]{1,0:T(8,128)S(1)} %get-tuple-element.14.sums_ref, f32[128,128]{1,0:T(8,128)S(1)} %get-tuple-element.15.stats_ref, bf16[1056,128]{1,0:T(8,128)(2,1)S(1)} %collective-permute-done.11.beside_ref), custom_call_target="tpu_custom_call" | custom-call | flops 1048576 | bytes 2097152 | tf_op jit(solution)/shard_map/merge/pallas_call | solution.py:399
  (2 shorter events, 0.0 us)
Async XLA Ops:
  0.8 14.6 %copy-start.1 = (bf16[128,1024]{1,0:T(8,128)(2,1)S(1)}, bf16[128,1024]{1,0:T(8,128)(2,1)}, u32[]{:S(2)}) copy-start(bf16[128,1024]{1,0:T(8,128)(2,1)} %queries_ref.1) | copy-start | bytes 786436
  0.8 22.3 %copy-start = (s32[64]{0:T(128)S(1)}, s32[64]{0:T(128)}, u32[]{:S(2)}) copy-start(s32[64]{0:T(128)} %order_ref.1) | copy-start | bytes 772
  0.8 5.1 %collective-permute-start = (bf16[128,256]{1,0:T(8,128)(2,1)S(1)}, bf16[128,256]{1,0:T(8,128)(2,1)S(1)}, u32[]{:S(2)}, u32[]{:S(2)}) collective-permute-start(bf16[128,256]{1,0:T(8,128)(2,1)S(1)} %pad_select_fusion), channel_id=1, source_target_pairs={{0,16},{1,3},{2,18},{3,5},{4,20},{5,7},{6,22},{7,1},{8,24},{9,11},... | collective-permute-start | bytes 196616 | tf_op jit(solution)/shard_map/ppermute | solution.py:51
  2.9 3.1 %collective-permute-start.1 = (bf16[128,256]{1,0:T(8,128)(2,1)S(1)}, bf16[128,256]{1,0:T(8,128)(2,1)S(1)}, u32[]{:S(2)}, u32[]{:S(2)}) collective-permute-start(bf16[128,256]{1,0:T(8,128)(2,1)S(1)} %pad_select_fusion), channel_id=1, source_target_pairs={{0,48},{1,7},{2,50},{3,1},{4,52},{5,3},{6,54},{7,5},{8,56},{9,15},... | collective-permute-start | bytes 196616 | tf_op jit(solution)/shard_map/ppermute | solution.py:51
  4.3 4.6 %collective-permute-start.2 = (bf16[128,256]{1,0:T(8,128)(2,1)S(1)}, bf16[128,256]{1,0:T(8,128)(2,1)S(1)}, u32[]{:S(2)}, u32[]{:S(2)}) collective-permute-start(bf16[128,256]{1,0:T(8,128)(2,1)S(1)} %pad_select_fusion), channel_id=1, source_target_pairs={{0,32},{1,5},{2,34},{3,7},{4,36},{5,1},{6,38},{7,3},{8,40},{9,13},... | collective-permute-start | bytes 196616 | tf_op jit(solution)/shard_map/ppermute | solution.py:51
  8.9 11.3 %collective-permute-start.4 = (bf16[512,256]{1,0:T(8,128)(2,1)S(1)}, bf16[512,256]{1,0:T(8,128)(2,1)S(1)}, u32[]{:S(2)}, u32[]{:S(2)}) collective-permute-start(bf16[512,256]{1,0:T(8,128)(2,1)S(1)} %pad_maximum_fusion.refs_0_), channel_id=1, source_target_pairs={{0,4},{1,33},{2,6},{3,35},{4,0},{5,37},{6,2},{7,39},{8,12},{9,41},... | collective-permute-start | bytes 786440 | tf_op jit(solution)/shard_map/ppermute | solution.py:51
  12.7 7.6 %collective-permute-start.6 = (bf16[512,256]{1,0:T(8,128)(2,1)S(1)}, bf16[512,256]{1,0:T(8,128)(2,1)S(1)}, u32[]{:S(2)}, u32[]{:S(2)}) collective-permute-start(bf16[512,256]{1,0:T(8,128)(2,1)S(1)} %pad_maximum_fusion.refs_0_), channel_id=1, source_target_pairs={{0,2},{1,17},{2,4},{3,19},{4,6},{5,21},{6,0},{7,23},{8,10},{9,25},... | collective-permute-start | bytes 786440 | tf_op jit(solution)/shard_map/ppermute | solution.py:51
  13.7 9.3 %collective-permute-start.7 = (bf16[512,256]{1,0:T(8,128)(2,1)S(1)}, bf16[512,256]{1,0:T(8,128)(2,1)S(1)}, u32[]{:S(2)}, u32[]{:S(2)}) collective-permute-start(bf16[512,256]{1,0:T(8,128)(2,1)S(1)} %pad_maximum_fusion.refs_0_), channel_id=1, source_target_pairs={{0,6},{1,49},{2,0},{3,51},{4,2},{5,53},{6,4},{7,55},{8,14},{9,57},... | collective-permute-start | bytes 786440 | tf_op jit(solution)/shard_map/ppermute | solution.py:51
  15.4 9.5 %collective-permute-start.10 = (bf16[128,1024]{1,0:T(8,128)(2,1)S(1)}, bf16[128,1024]{1,0:T(8,128)(2,1)S(1)}, u32[]{:S(2)}, u32[]{:S(2)}) collective-permute-start(bf16[128,1024]{1,0:T(8,128)(2,1)S(1)} %copy-done.1), channel_id=1, source_target_pairs={{0,8},{1,9},{2,10},{3,11},{4,12},{5,13},{6,14},{7,15},{8,0},{9,1},... | collective-permute-start | bytes 786440 | tf_op jit(solution)/shard_map/ppermute | solution.py:51
  16.7 10.1 %collective-permute-start.3 = (bf16[512,256]{1,0:T(8,128)(2,1)S(1)}, bf16[512,256]{1,0:T(8,128)(2,1)S(1)}, u32[]{:S(2)}, u32[]{:S(2)}) collective-permute-start(bf16[512,256]{1,0:T(8,128)(2,1)S(1)} %pad_maximum_fusion.refs_0_), channel_id=1, source_target_pairs={{0,1},{1,0},{2,3},{3,2},{4,5},{5,4},{6,7},{7,6},{8,9},{9,8},{10,11... | collective-permute-start | bytes 786440 | tf_op jit(solution)/shard_map/ppermute | solution.py:51
  20.2 8.8 %collective-permute-start.5 = (bf16[512,256]{1,0:T(8,128)(2,1)S(1)}, bf16[512,256]{1,0:T(8,128)(2,1)S(1)}, u32[]{:S(2)}, u32[]{:S(2)}) collective-permute-start(bf16[512,256]{1,0:T(8,128)(2,1)S(1)} %collective-permute-done.4.refs_2_.refs_1_), channel_id=1, source_target_pairs={{0,1},{1,0},{2,3},{3,2},{4,5},{5,4},{6,7},{7,6},{8,9},{9,8},{10,11... | collective-permute-start | bytes 786440 | tf_op jit(solution)/shard_map/ppermute | solution.py:51
  20.3 11.5 %collective-permute-start.8 = (bf16[512,256]{1,0:T(8,128)(2,1)S(1)}, bf16[512,256]{1,0:T(8,128)(2,1)S(1)}, u32[]{:S(2)}, u32[]{:S(2)}) collective-permute-start(bf16[512,256]{1,0:T(8,128)(2,1)S(1)} %collective-permute-done.6.refs_4_.refs_1_), channel_id=1, source_target_pairs={{0,1},{1,0},{2,3},{3,2},{4,5},{5,4},{6,7},{7,6},{8,9},{9,8},{10,11... | collective-permute-start | bytes 786440 | tf_op jit(solution)/shard_map/ppermute | solution.py:51
  23.1 8.7 %collective-permute-start.9 = (bf16[512,256]{1,0:T(8,128)(2,1)S(1)}, bf16[512,256]{1,0:T(8,128)(2,1)S(1)}, u32[]{:S(2)}, u32[]{:S(2)}) collective-permute-start(bf16[512,256]{1,0:T(8,128)(2,1)S(1)} %collective-permute-done.7.refs_5_.refs_2_), channel_id=1, source_target_pairs={{0,1},{1,0},{2,3},{3,2},{4,5},{5,4},{6,7},{7,6},{8,9},{9,8},{10,11... | collective-permute-start | bytes 786440 | tf_op jit(solution)/shard_map/ppermute | solution.py:51
  34.3 7.8 %collective-permute-start.11 = (bf16[1056,128]{1,0:T(8,128)(2,1)S(1)}, bf16[1056,128]{1,0:T(8,128)(2,1)S(1)}, u32[]{:S(2)}, u32[]{:S(2)}) collective-permute-start(bf16[1056,128]{1,0:T(8,128)(2,1)S(1)} %shard_map.50), channel_id=1, source_target_pairs={{0,8},{1,9},{2,10},{3,11},{4,12},{5,13},{6,14},{7,15},{8,0},{9,1},... | collective-permute-start | bytes 811016 | tf_op jit(solution)/shard_map/ppermute | solution.py:51
